TPU v7x, 32 devices: a whole 2x2x4 slice. The times are simulated.
32 devices in a mesh: seq: 16 (over z, y, core), mp: 2 (over x).
Axes of the slice: x: 2, y: 2, z: 4, core: 2. Of those that a mesh axis runs over, the one named last changes fastest.
Arguments:
- hidden: bfloat16 [4096, 2048], P('seq'), may hold values from -6 to 6
- ids: int32 [4096], P('seq'), may hold values from 0 to 4, as said below
- w_value: bfloat16 [2048, 2048], P(None, 'mp'), may hold values from -0.125 to 0.125
- w_bc: bfloat16 [2048, 2, 64], P(None, 'mp'), may hold values from -0.015625 to 0.015625
- w_step: bfloat16 [2048, 16], P(None, 'mp'), may hold values from -0.125 to 0.125
- step_bias: float32 [16], P('mp'), may hold values from -1 to 1
- decay_log: float32 [16], P('mp'), may hold values from -12 to -2
- skip: float32 [16], P('mp'), may hold values from 0.5 to 1.5
- norm_gain: float32 [2048], P('mp'), may hold values from 0.1 to 1.9
- w_out: bfloat16 [2048, 2048], P('mp'), may hold values from -0.125 to 0.125
- cotangent: bfloat16 [4096, 2048], P('seq'), may hold values from -6 to 6
Outputs:
- out: bfloat16 [4096, 2048], P('seq', 'mp')
- d_hidden: bfloat16 [4096, 2048], P('seq', 'mp')
Inputs may be any that keep to these rules, and one draw needn't show every extreme that they name: `ids`: 4 marks an unknown base (N); such bases come in runs.
All inputs are finite; a program needn't handle non-finite values.
Results may differ from a plain program's by a relative error of at most 0.014.
Values may be sent and summed in bfloat16 or wider, within the bound.
A program may use at most 320 MiB of HBM per device.

v0:
```python
from functools import partial

import jax
import jax.numpy as jnp
from jax import lax
from jax.experimental import pallas as pl
from jax.experimental.pallas import tpu as pltpu
from jax.sharding import PartitionSpec as P

f32, bf16 = jnp.float32, jnp.bfloat16
epsilon = 1e-05
LANES = 128
MXU_NN = (((1,), (0,)), ((), ()))
MXU_NT = (((1,), (1,)), ((), ()))
MXU_TN = (((0,), (0,)), ((), ()))
PARAMS = pltpu.CompilerParams(vmem_limit_bytes=56 * 1024 * 1024)


def dot(a, b, dims=MXU_NN, precision=None):
    return lax.dot_general(a, b, dims, preferred_element_type=f32, precision=precision)


def iota2(shape, axis):
    return lax.broadcasted_iota(jnp.int32, shape, axis)


def exchange_matrix():
    return (iota2((LANES, LANES), 0) + iota2((LANES, LANES), 1) == LANES - 1).astype(bf16)


def sources_kernel(hidden_ref, cot_ref, ids_ref, src_ref, grad_ref):
    tiles = hidden_ref.shape[1] // LANES
    mirror = exchange_matrix()
    known = ids_ref[...] != 4
    src_ref[0] = hidden_ref[...]
    for k in range(tiles):
        there = pl.ds((tiles - 1 - k) * LANES, LANES)
        here = pl.ds(k * LANES, LANES)
        src_ref[1, :, there] = dot(hidden_ref[:, here], mirror).astype(bf16)
        tile = jnp.where(known, cot_ref[:, here].astype(f32), 0.0).astype(bf16)
        grad_ref[0, :, here] = tile
        grad_ref[1, :, there] = dot(tile, mirror).astype(bf16)


def merge_kernel(main_ref, mirrored_ref, out_ref):
    tiles = out_ref.shape[1] // LANES
    mirror = exchange_matrix()
    for k in range(tiles):
        here = pl.ds(k * LANES, LANES)
        there = pl.ds((tiles - 1 - k) * LANES, LANES)
        flipped = dot(mirrored_ref[:, there].astype(bf16), mirror)
        out_ref[:, here] = (main_ref[:, here] + flipped).astype(out_ref.dtype)


def prepare(aux, consts):
    length = aux.shape[0]
    shifted = aux + consts[0:1]
    dt = jnp.maximum(shifted, 0.0) + jnp.log1p(jnp.exp(-jnp.abs(shifted)))
    la = -jnp.exp(consts[1:2]) * dt
    lower = (iota2((length, length), 0) >= iota2((length, length), 1)).astype(f32)
    cum = dot(lower, la, precision=lax.Precision.HIGHEST)
    return shifted, dt, la, cum, cum - la


def put_rows(parcel_ref, h, which, value):
    count, _, _, rows, _ = parcel_ref.shape
    per = value.shape[0] // rows
    for k in range(per):
        parcel_ref[h * per + k, 0, which] = value[k * rows : (k + 1) * rows].astype(bf16)


def put_decay(parcel_ref, h, heads, decay):
    count, _, _, rows, _ = parcel_ref.shape
    per = count // heads
    wide = jnp.broadcast_to(decay, (rows, LANES))
    main = wide.astype(bf16).astype(f32)
    packed = jnp.where(iota2((rows, LANES), 0) < rows // 2, main, wide - main).astype(bf16)
    for k in range(per):
        parcel_ref[h * per + k, 0, 2] = packed


def take_rows(parcel_ref, h, heads, which):
    per = parcel_ref.shape[0] // heads
    pieces = [parcel_ref[h * per + k, 0, which].astype(f32) for k in range(per)]
    return jnp.concatenate(pieces, axis=0)


def exchange_kernel(
    upward, parcel_ref, out_ref, got, back, final, send_out, recv_out, send_back, recv_back
):
    count = parcel_ref.shape[0]
    me = lax.axis_index("seq")
    barrier = pltpu.get_barrier_semaphore()
    mesh_id = pl.DeviceIdType.MESH

    def peer_of(hop):
        return lax.rem(me + hop, count)

    def greet(hop, none):
        pl.semaphore_signal(
            barrier, inc=1, device_id={"seq": peer_of(hop)}, device_id_type=mesh_id
        )
        return none

    lax.fori_loop(1, count, greet, 0)
    pl.semaphore_wait(barrier, count - 1)

    def outward(hop):
        return pltpu.make_async_remote_copy(
            src_ref=parcel_ref.at[peer_of(hop)], dst_ref=got.at[me],
            send_sem=send_out.at[hop], recv_sem=recv_out.at[hop],
            device_id={"seq": peer_of(hop)}, device_id_type=mesh_id,
        )

    def homeward(hop):
        return pltpu.make_async_remote_copy(
            src_ref=back.at[peer_of(hop)], dst_ref=final.at[me],
            send_sem=send_back.at[hop], recv_sem=recv_back.at[hop],
            device_id={"seq": peer_of(hop)}, device_id_type=mesh_id,
        )

    def start(copy):
        def step(hop, none):
            copy(hop).start()
            return none

        lax.fori_loop(1, count, step, 0)

    def finish(copy):
        def step(hop, none):
            copy(hop).wait()
            return none

        lax.fori_loop(1, count, step, 0)

    start(outward)
    got[me] = parcel_ref[me]
    finish(outward)
    rows = got.shape[3]
    zero = jnp.zeros((2, rows, LANES), f32)

    def scan(i, totals):
        result = []
        for which in range(2):
            j = count - 1 - i if (which == 1) != upward else i
            total = totals[which]
            back[j, :, which] = total.astype(bf16)
            packed = got[j, :, 2].astype(f32)
            decay = packed[:, :1] + packed[:, rows // 2 : rows // 2 + 1]
            result.append(decay * total + got[j, :, which].astype(f32))
        return tuple(result)

    lax.fori_loop(0, count, scan, (zero, zero))
    start(homeward)
    final[me] = back[me]
    finish(homeward)
    out_ref[...] = final[...]


def exchange(parcels, upward, collective_id):
    count, streams, _, rows, _ = parcels.shape
    carried = (count, streams, 2, rows, LANES)
    return pl.pallas_call(
        partial(exchange_kernel, upward),
        in_specs=[pl.BlockSpec(memory_space=pltpu.VMEM)],
        out_specs=pl.BlockSpec(memory_space=pltpu.VMEM),
        out_shape=shape_of(bf16, *carried),
        scratch_shapes=[
            pltpu.VMEM(parcels.shape, bf16), pltpu.VMEM(carried, bf16), pltpu.VMEM(carried, bf16),
        ] + [pltpu.SemaphoreType.DMA((count,))] * 4,
        compiler_params=pltpu.CompilerParams(
            collective_id=collective_id, has_side_effects=True,
            vmem_limit_bytes=32 * 1024 * 1024,
        ),
    )(parcels)


def ends_kernel(heads, state, aux_ref, consts_ref, x_ref, st_ref):
    aux = aux_ref[0]
    length = aux.shape[0]
    _, dt, la, cum, exc = prepare(aux, consts_ref[...])
    cum_t, exc_t, dt_t = cum.T[:heads], exc.T[:heads], dt.T[:heads]
    b_t = aux.astype(bf16).astype(f32).T[LANES - 2 * state : LANES - state]
    end = cum_t[:, length - 1 : length]
    w_f = jnp.exp(end - cum_t) * dt_t
    w_r = jnp.exp(exc_t) * dt_t
    for h in range(heads):
        left = jnp.concatenate([b_t * w_f[h : h + 1], b_t * w_r[h : h + 1]], axis=0).astype(bf16)
        both = dot(left, x_ref[0, :, pl.ds(h * LANES, LANES)])
        put_rows(st_ref, h, 0, both[:state])
        put_rows(st_ref, h, 1, both[state:])
        put_decay(st_ref, h, heads, jnp.exp(end[h : h + 1]))


def outputs_kernel(
    heads, state,
    aux_ref, consts_ref, x_ref, dz_ref, gain_ref, start_ref,
    z_ref, dy_ref, adj_ref, y_scr,
):
    aux, consts = aux_ref[0], consts_ref[...]
    length = aux.shape[0]
    _, dt, la, cum, exc = prepare(aux, consts)
    cum_t, exc_t, dt_t = cum.T[:heads], exc.T[:heads], dt.T[:heads]
    end_t = cum_t[:, length - 1 : length]
    rounded = aux.astype(bf16)
    b_m = rounded[:, LANES - 2 * state : LANES - state]
    c_m = rounded[:, LANES - state :]
    c32 = c_m.astype(f32)
    c_t = rounded.astype(f32).T[LANES - state :]
    scores = dot(c_m, b_m, MXU_NT)
    rows, cols = iota2((length, length), 0), iota2((length, length), 1)
    grow_f = jnp.exp(cum)
    grow_r = jnp.exp(cum[length - 1 : length] - exc)
    sq_f = jnp.zeros((length, 1), f32)
    sq_r = jnp.zeros((length, 1), f32)
    for h in range(heads):
        at = pl.ds(h * LANES, LANES)
        one = slice(h, h + 1)
        spread = jnp.where(
            rows >= cols, cum[:, one] - cum_t[one], exc_t[one] - exc[:, one]
        )
        mix = jnp.exp(spread) * scores * dt_t[one]
        low = jnp.where(rows >= cols, mix, 0.0).astype(bf16)
        high = jnp.where(rows <= cols, mix, 0.0).astype(bf16)
        x_h = x_ref[0, :, at]
        direct = consts[2:3, one] * x_h.astype(f32)
        y_f = dot(low, x_h) + direct
        y_f += dot((c32 * grow_f[:, one]).astype(bf16), take_rows(start_ref, h, heads, 0).astype(bf16))
        y_r = dot(high, x_h) + direct
        y_r += dot((c32 * grow_r[:, one]).astype(bf16), take_rows(start_ref, h, heads, 1).astype(bf16))
        y_scr[0, :, at] = y_f
        y_scr[1, :, at] = y_r
        sq_f += jnp.sum(y_f * y_f, axis=1, keepdims=True)
        sq_r += jnp.sum(y_r * y_r, axis=1, keepdims=True)
    share = 1.0 / (heads * LANES)
    rs_f = lax.rsqrt(sq_f * share + epsilon)
    rs_r = lax.rsqrt(sq_r * share + epsilon)
    m_f = jnp.zeros((length, 1), f32)
    m_r = jnp.zeros((length, 1), f32)
    for h in range(heads):
        at = pl.ds(h * LANES, LANES)
        gain = gain_ref[:, at]
        n_f, n_r = y_scr[0, :, at] * rs_f, y_scr[1, :, at] * rs_r
        z_ref[0, :, at] = (n_f * gain + n_r * gain).astype(bf16)
        g = dz_ref[0, :, at].astype(f32) * gain
        m_f += jnp.sum(g * n_f, axis=1, keepdims=True)
        m_r += jnp.sum(g * n_r, axis=1, keepdims=True)
    m_f, m_r = m_f * share, m_r * share
    out_f = jnp.exp(cum_t)
    out_r = jnp.exp(end_t - exc_t)
    for h in range(heads):
        at = pl.ds(h * LANES, LANES)
        one = slice(h, h + 1)
        g = dz_ref[0, :, at].astype(f32) * gain_ref[:, at]
        d_f = (rs_f * (g - y_scr[0, :, at] * rs_f * m_f)).astype(bf16)
        d_r = (rs_r * (g - y_scr[1, :, at] * rs_r * m_r)).astype(bf16)
        dy_ref[0, 0, :, at] = d_f
        dy_ref[0, 1, :, at] = d_r
        put_rows(adj_ref, h, 0, dot((c_t * out_f[one]).astype(bf16), d_f))
        put_rows(adj_ref, h, 1, dot((c_t * out_r[one]).astype(bf16), d_r))
        put_decay(adj_ref, h, heads, jnp.exp(end_t[one]))


def grads_kernel(
    heads, state,
    aux_ref, consts_ref, x_ref, dy_ref, start_ref, own_ref, in_ref,
    dx_ref, tail_ref,
):
    aux, consts = aux_ref[0], consts_ref[...]
    length = aux.shape[0]
    shifted, dt, la, cum, exc = prepare(aux, consts)
    cum_t, exc_t = cum.T[:heads], exc.T[:heads]
    end = cum[length - 1 : length]
    rounded = aux.astype(bf16)
    b_m = rounded[:, LANES - 2 * state : LANES - state]
    c_m = rounded[:, LANES - state :]
    b32, c32 = b_m.astype(f32), c_m.astype(f32)
    scores_t = dot(b_m, c_m, MXU_NT)
    rows, cols = iota2((length, length), 0), iota2((length, length), 1)
    lane = iota2((length, LANES), 1)
    lane_row = iota2((1, LANES), 1)
    grow_f, grow_r = jnp.exp(cum), jnp.exp(end - exc)
    tail_f, tail_r = jnp.exp(end - cum), jnp.exp(exc)
    end_decay = jnp.exp(end)
    zero = jnp.zeros((length, LANES), f32)
    into_f, into_r = zero, zero
    carry_f, carry_r = zero, zero
    total = jnp.zeros((1, LANES), f32)
    from_f, from_r = [], []
    d_scores = jnp.zeros((length, length), f32)
    d_b = jnp.zeros((length, state), f32)
    d_c = jnp.zeros((length, state), f32)
    for h in range(heads):
        at = pl.ds(h * LANES, LANES)
        one = slice(h, h + 1)
        x_h, d_f, d_r = x_ref[0, :, at], dy_ref[0, 0, :, at], dy_ref[0, 1, :, at]
        s_f, s_r = take_rows(start_ref, h, heads, 0), take_rows(start_ref, h, heads, 1)
        a_f, a_r = take_rows(in_ref, h, heads, 0), take_rows(in_ref, h, heads, 1)
        dt_h = dt[:, one]
        decay = jnp.exp(
            jnp.where(cols >= rows, cum_t[one] - cum[:, one], exc[:, one] - exc_t[one])
        )
        weight = decay * scores_t
        w_f = jnp.where(cols >= rows, weight, 0.0)
        w_r = jnp.where(cols <= rows, weight, 0.0)
        p_f = dot(x_h, d_f, MXU_NT)
        p_r = dot(x_h, d_r, MXU_NT)
        picked = jnp.where(cols >= rows, p_f, 0.0) + jnp.where(cols <= rows, p_r, 0.0)
        d_scores += decay * picked * dt_h
        n_f, n_r = w_f * p_f, w_r * p_r
        from_f.append(jnp.sum(n_f * dt_h, axis=0, keepdims=True))
        from_r.append(jnp.sum(n_r * dt_h, axis=0, keepdims=True))
        in_f = jnp.sum(n_f, axis=1, keepdims=True)
        in_r = jnp.sum(n_r, axis=1, keepdims=True)
        d_u = dot(w_f.astype(bf16), d_f) + dot(w_r.astype(bf16), d_r)
        d_u += dot((b32 * tail_f[:, one]).astype(bf16), a_f.astype(bf16))
        d_u += dot((b32 * tail_r[:, one]).astype(bf16), a_r.astype(bf16))
        v_f = dot(x_h, a_f.astype(bf16), MXU_NT) * tail_f[:, one]
        v_r = dot(x_h, a_r.astype(bf16), MXU_NT) * tail_r[:, one]
        d_b += (v_f + v_r) * dt_h
        in_f += jnp.sum(v_f * b32, axis=1, keepdims=True)
        in_r += jnp.sum(v_r * b32, axis=1, keepdims=True)
        u_f = dot(d_f, s_f.astype(bf16), MXU_NT) * grow_f[:, one]
        u_r = dot(d_r, s_r.astype(bf16), MXU_NT) * grow_r[:, one]
        d_c += u_f + u_r
        c_f = jnp.sum(u_f * c32, axis=1, keepdims=True)
        c_r = jnp.sum(u_r * c32, axis=1, keepdims=True)
        skipped = consts[2:3, one] * (d_f.astype(f32) + d_r.astype(f32))
        dx_ref[0, :, at] = (dt_h * d_u + skipped).astype(bf16)
        into_f = jnp.where(lane == h, in_f, into_f)
        into_r = jnp.where(lane == h, in_r, into_r)
        carry_f = jnp.where(lane == h, c_f, carry_f)
        carry_r = jnp.where(lane == h, c_r, carry_r)
        ending = a_f * (end_decay[:, one] * s_f + take_rows(own_ref, h, heads, 0))
        ending += a_r * (end_decay[:, one] * s_r)
        ended = jnp.sum(jnp.sum(ending, axis=1, keepdims=True), axis=0, keepdims=True)
        ended += jnp.sum(c_r, axis=0, keepdims=True)
        total = jnp.where(lane_row == h, ended, total)
    pad = [jnp.zeros((LANES - heads, length), f32)]
    given_f = jnp.concatenate(from_f + pad, axis=0).T + carry_f
    given_r = jnp.concatenate(from_r + pad, axis=0).T + carry_r
    d_cum = given_f - dt * into_f
    d_exc = dt * into_r - given_r
    upper = (rows <= cols).astype(f32)
    d_la = dot(upper, d_cum + d_exc, precision=lax.Precision.HIGHEST) - d_exc + total
    d_dt = into_f + into_r - jnp.exp(consts[1:2]) * d_la
    d_raw = jnp.where(lane < heads, d_dt * jax.nn.sigmoid(shifted), 0.0)
    d_scores = d_scores.astype(bf16)
    d_b += dot(d_scores, c_m)
    d_c += dot(d_scores, b_m, MXU_TN)
    tail_ref[0] = jnp.concatenate(
        [d_raw[:, : LANES - 2 * state], d_b, d_c], axis=1
    ).astype(bf16)


def by_stream(*shape):
    return pl.BlockSpec((1,) + shape, lambda s: (s,) + (0,) * len(shape))


def gathered(count, *shape):
    return pl.BlockSpec((count, 1) + shape, lambda s: (0, s) + (0,) * len(shape))


def shared(*shape):
    return pl.BlockSpec(shape, lambda s: (0,) * len(shape))


def shape_of(dtype, *shape):
    return jax.ShapeDtypeStruct(shape, dtype)


def merge(main, mirrored, dtype):
    return pl.pallas_call(
        merge_kernel, out_shape=shape_of(dtype, *main.shape), compiler_params=PARAMS
    )(main, mirrored)


def out_share(z, w_out, part, parts, dtype):
    width = w_out.shape[1] // parts
    main = lax.dynamic_slice_in_dim(w_out, part * width, width, 1)
    mirrored = lax.dynamic_slice_in_dim(w_out, (parts - 1 - part) * width, width, 1)
    return merge(dot(z[0], main), dot(z[1], mirrored), dtype)


def hidden_share(dx, tail, w_value, w_side, part, parts, dtype):
    width = w_value.shape[0] // parts
    terms = []
    for stream, place in ((0, part), (1, parts - 1 - part)):
        value = lax.dynamic_slice_in_dim(w_value, place * width, width, 0)
        side = lax.dynamic_slice_in_dim(w_side, place * width, width, 0)
        terms.append(dot(dx[stream], value, MXU_NT) + dot(tail[stream], side, MXU_NT))
    return merge(*terms, dtype)


def send_on(leaving, hop, parts):
    return lax.ppermute(leaving, "mp", [(i, (i + hop) % parts) for i in range(parts)])


def per_device(
    hidden, ids, w_value, w_bc, w_step, step_bias, decay_log, skip, norm_gain, w_out, cotangent
):
    length, width = hidden.shape
    heads = w_step.shape[1]
    inner = w_value.shape[1]
    state = w_bc.shape[2] // 2
    assert w_bc.shape[1] == 1 and inner == heads * LANES
    count, parts = lax.axis_size("seq"), lax.axis_size("mp")
    sources, grads = pl.pallas_call(
        sources_kernel,
        out_shape=(shape_of(bf16, 2, length, width),) * 2,
        compiler_params=PARAMS,
    )(hidden, cotangent, ids[:, None])
    sources = sources.reshape(2 * length, width)
    grads = grads.reshape(2 * length, width)
    spare = jnp.zeros((width, LANES - heads - 2 * state), bf16)
    w_side = jnp.concatenate([w_step, spare, w_bc.reshape(width, -1)], axis=1)
    consts = jnp.pad(
        jnp.stack([step_bias, decay_log, skip]), ((0, 5), (0, LANES - heads))
    )
    aux = dot(sources, w_side).reshape(2, length, LANES)
    x = dot(sources, w_value).astype(bf16).reshape(2, length, inner)
    assert count % heads == 0 and (heads * state) % count == 0
    rows = heads * state // count
    parcel = (count, 2, 3, rows, LANES)
    states = pl.pallas_call(
        partial(ends_kernel, heads, state),
        grid=(2,),
        in_specs=[by_stream(length, LANES), shared(8, LANES), by_stream(length, inner)],
        out_specs=gathered(count, 3, rows, LANES),
        out_shape=shape_of(bf16, *parcel),
        compiler_params=PARAMS,
    )(aux, consts, x)
    starts = exchange(states, False, 0)
    dz = dot(grads, w_out, MXU_NT).astype(bf16).reshape(2, length, inner)
    z, dy, adjoint = pl.pallas_call(
        partial(outputs_kernel, heads, state),
        grid=(2,),
        in_specs=[
            by_stream(length, LANES), shared(8, LANES), by_stream(length, inner),
            by_stream(length, inner), shared(1, inner), gathered(count, 2, rows, LANES),
        ],
        out_specs=[
            by_stream(length, inner), by_stream(2, length, inner),
            gathered(count, 3, rows, LANES),
        ],
        out_shape=(
            shape_of(bf16, 2, length, inner), shape_of(bf16, 2, 2, length, inner),
            shape_of(bf16, *parcel),
        ),
        scratch_shapes=[pltpu.VMEM((2, length, inner), f32)],
        compiler_params=PARAMS,
    )(aux, consts, x, dz, norm_gain[None], starts)
    mine = lax.axis_index("mp")
    hops = range(1, parts)
    leaving = [out_share(z, w_out, lax.rem(mine + hop, parts), parts, bf16) for hop in hops]
    adjoint, leaving = lax.optimization_barrier((adjoint, leaving))
    out_received = [send_on(share, hop, parts) for hop, share in zip(hops, leaving)]
    arriving = exchange(adjoint, True, 1)
    dx, tail = pl.pallas_call(
        partial(grads_kernel, heads, state),
        grid=(2,),
        in_specs=[
            by_stream(length, LANES), shared(8, LANES), by_stream(length, inner),
            by_stream(2, length, inner), gathered(count, 2, rows, LANES),
            gathered(count, 3, rows, LANES), gathered(count, 2, rows, LANES),
        ],
        out_specs=[by_stream(length, inner), by_stream(length, LANES)],
        out_shape=(shape_of(bf16, 2, length, inner), shape_of(bf16, 2, length, LANES)),
        cost_estimate=pl.CostEstimate(
            flops=24 * length * length * inner, bytes_accessed=16 * length * inner,
            transcendentals=2 * heads * length * length,
        ),
        compiler_params=PARAMS,
    )(aux, consts, x, dy, starts, states, arriving)
    dx, tail, out_received = lax.optimization_barrier((dx, tail, out_received))
    leaving = [
        hidden_share(dx, tail, w_value, w_side, lax.rem(mine + hop, parts), parts, bf16)
        for hop in hops
    ]
    dx, tail, z, leaving = lax.optimization_barrier((dx, tail, z, leaving))
    received = [send_on(share, hop, parts) for hop, share in zip(hops, leaving)]
    out = out_share(z, w_out, mine, parts, f32)
    d_hidden = hidden_share(dx, tail, w_value, w_side, mine, parts, f32)
    for share in out_received:
        out += share.astype(f32)
    for share in received:
        d_hidden += share.astype(f32)
    return (out.astype(bf16), d_hidden.astype(bf16))


def solution(mesh):
    in_specs = (
        P("seq", None),
        P("seq"),
        P(None, "mp"),
        P(None, "mp", None),
        P(None, "mp"),
        P("mp"),
        P("mp"),
        P("mp"),
        P("mp"),
        P("mp", None),
        P("seq", None),
    )
    out_specs = (P("seq", "mp"), P("seq", "mp"))
    return jax.shard_map(
        per_device, mesh=mesh, in_specs=in_specs, out_specs=out_specs, check_vma=False
    )
```

profile of v0, /device:TPU:0, one launch (start us, length us, event | category | flops | bytes accessed | tf_op | source)
XLA Modules:
  0.0 144.4 jit_solution(18221209394790532006)
XLA Ops:
  0.6 1.2 copy.16
  1.9 1.0 copy.17
  2.9 1.5 %copy.15.ids_ref = s32[256,1]{1,0:T(8,128)} copy(s32[256,1]{0,1:T(1,128)} %bitcast.61) | data formatting | bytes 2048 | tf_op jit(solution)/shard_map/broadcast_in_dim | solution.py:412
  4.8 4.6 %shard_map.122 = (bf16[2,256,2048]{2,1,0:T(8,128)(2,1)}, bf16[2,256,2048]{2,1,0:T(8,128)(2,1)}) custom-call(bf16[256,2048]{1,0:T(8,128)(2,1)} %hidden_ref.1, bf16[256,2048]{1,0:T(8,128)(2,1)} %cot_ref.1, s32[256,1]{1,0:T(8,128)} %copy.15.ids_ref), custom_call_target="tpu_custom_call" | custom-call | tf_op jit(solution)/shard_map/pallas_call | solution.py:408
  9.4 3.0 %fusion.36.aux_ref = f32[2,256,128]{2,1,0:T(8,128)} fusion(bf16[2,256,2048]{2,1,0:T(8,128)(2,1)} %get-tuple-element.18, bf16[2048,128]{1,0:T(8,128)(2,1)S(1)} %pad_maximum_fusion), kind=kOutput, calls=%fused_computation.33 | convolution fusion | flops 268435456 | bytes 2883584 | tf_op jit(solution)/shard_map/dot_general | solution.py:20
  12.5 5.1 %convolution_convert_fusion.1 = bf16[512,1024]{1,0:T(8,128)(2,1)} fusion(bf16[512,2048]{1,0:T(8,128)(2,1)} %bitcast.57, bf16[2048,1024]{1,0:T(8,128)(2,1)S(1)} %copy-done.4), kind=kOutput, calls=%fused_computation.17 | convolution fusion | flops 2148007936 | bytes 7340032 | tf_op jit(solution)/shard_map/dot_general | solution.py:20
  18.2 3.6 %shard_map.123.parcel_ref.own_ref = bf16[16,2,3,16,128]{4,3,2,1,0:T(8,128)(2,1)} custom-call(f32[2,256,128]{2,1,0:T(8,128)} %fusion.36.aux_ref, f32[8,128]{1,0:T(8,128)} %select_maximum_fusion.consts_ref, bf16[2,256,1024]{2,1,0:T(8,128)(2,1)} %bitcast.54), custom_call_target="tpu_custom_call" | custom-call | tf_op jit(solution)/shard_map/pallas_call | solution.py:425
  21.7 1.0 copy-done
  22.7 21.7 %shard_map.124.start_ref = bf16[16,2,2,16,128]{4,3,2,1,0:T(8,128)(2,1)S(1)} custom-call(bf16[16,2,3,16,128]{4,3,2,1,0:T(8,128)(2,1)S(1)} %copy-done), custom_call_target="tpu_custom_call" | custom-call | tf_op jit(solution)/shard_map/pallas_call | solution.py:163
  44.4 0.7 copy-done.1
  45.1 5.7 %convolution_convert_fusion = bf16[512,1024]{1,0:T(8,128)(2,1)} fusion(bf16[512,2048]{1,0:T(8,128)(2,1)S(1)} %bitcast.65, bf16[1024,2048]{1,0:T(8,128)(2,1)} %param.20), kind=kOutput, calls=%fused_computation.16 | convolution fusion | flops 2148007936 | bytes 7340032 | tf_op jit(solution)/shard_map/dot_general | solution.py:20
  50.8 14.6 %shard_map.125 = (bf16[2,256,1024]{2,1,0:T(8,128)(2,1)}, bf16[2,2,256,1024]{3,2,1,0:T(8,128)(2,1)}, bf16[16,2,3,16,128]{4,3,2,1,0:T(8,128)(2,1)}) custom-call(f32[2,256,128]{2,1,0:T(8,128)} %fusion.36.aux_ref, f32[8,128]{1,0:T(8,128)} %select_maximum_fusion.consts_ref, bf16[2,256,1024]{2,1,0:T(8,128)(2,1)} %bitcast.55, bf16[2,256,1024]{2,1,0:T(8,128)(2,1)} %bitcast.59, ...), custom_call_target="tpu_custom_call" | custom-call | tf_op jit(solution)/shard_map/pallas_call | solution.py:435
  65.4 2.8 %fusion.12.mirrored_ref = f32[256,1024]{1,0:T(8,128)} fusion(bf16[1024,2048]{1,0:T(8,128)(2,1)S(1)} %copy-done.6, s32[]{:T(128)S(6)} %select_n.9, bf16[2,256,1024]{2,1,0:T(8,128)(2,1)} %get-tuple-element.29), kind=kOutput, calls=%fused_computation.12 | convolution fusion | flops 536870912 | bytes 3670020 | tf_op jit(solution)/shard_map/dot_general | solution.py:20
  68.2 3.3 %fusion.14.main_ref = f32[256,1024]{1,0:T(8,128)} fusion(bf16[1024,2048]{1,0:T(8,128)(2,1)} %param.20, s32[]{:T(128)S(6)} %select_n.8, bf16[2,256,1024]{2,1,0:T(8,128)(2,1)S(1)} %copy-done.11), kind=kOutput, calls=%fused_computation.14 | convolution fusion | flops 536870912 | bytes 3670020 | tf_op jit(solution)/shard_map/dot_general | solution.py:20
  71.5 2.7 %shard_map.126 = bf16[256,1024]{1,0:T(8,128)(2,1)} custom-call(f32[256,1024]{1,0:T(8,128)} %fusion.14.main_ref, f32[256,1024]{1,0:T(8,128)} %fusion.12.mirrored_ref), custom_call_target="tpu_custom_call" | custom-call | tf_op jit(solution)/shard_map/pallas_call | solution.py:373
  74.2 1.5 %collective-permute-start = (bf16[256,1024]{1,0:T(8,128)(2,1)}, bf16[256,1024]{1,0:T(8,128)(2,1)S(1)}, u32[]{:S(2)}, u32[]{:S(2)}) collective-permute-start(bf16[256,1024]{1,0:T(8,128)(2,1)} %shard_map.126), channel_id=1, source_target_pairs={{0,1},{1,0},{2,3},{3,2},{4,5},{5,4},{6,7},{7,6},{8,9},{9,8},{10,11... | collective-permute-start | bytes 1572872 | tf_op jit(solution)/shard_map/ppermute | solution.py:396
  75.7 20.7 %shard_map.127.in_ref = bf16[16,2,2,16,128]{4,3,2,1,0:T(8,128)(2,1)S(1)} custom-call(bf16[16,2,3,16,128]{4,3,2,1,0:T(8,128)(2,1)S(1)} %copy-done.2), custom_call_target="tpu_custom_call" | custom-call | tf_op jit(solution)/shard_map/pallas_call | solution.py:163
  97.1 19.7 %shard_map.128 = (bf16[2,256,1024]{2,1,0:T(8,128)(2,1)}, bf16[2,256,128]{2,1,0:T(8,128)(2,1)}) custom-call(f32[2,256,128]{2,1,0:T(8,128)} %fusion.36.aux_ref, f32[8,128]{1,0:T(8,128)} %select_maximum_fusion.consts_ref, bf16[2,256,1024]{2,1,0:T(8,128)(2,1)} %bitcast.56, bf16[2,2,256,1024]{3,2,1,0:T(8,128)(2,1)} %get-tuple-element.20.dy_ref, ...), custom_call_target="tpu_custom_call" | custom-call | flops 1610612736 | bytes 4194304 | tf_op jit(solution)/shard_map/pallas_call | solution.py:459
  116.9 1.2 fusion.50
  118.1 1.1 fusion.52
  119.3 1.7 %fusion.19.mirrored_ref = f32[256,1024]{1,0:T(8,128)} fusion(f32[256,1024]{1,0:T(8,128)S(1)} %fusion.50, bf16[2048,1024]{1,0:T(8,128)(2,1)S(1)} %copy-done.5, s32[]{:T(128)S(6)} %select_n.9, bf16[2,256,1024]{2,1,0:T(8,128)(2,1)S(1)} %copy-done.9), kind=kOutput, calls=%fused_computation.19 | convolution fusion | flops 537133056 | bytes 4718596 | tf_op jit(solution)/shard_map/dot_general | solution.py:20
  121.0 1.8 %fusion.16.main_ref = f32[256,1024]{1,0:T(8,128)} fusion(f32[256,1024]{1,0:T(8,128)S(1)} %fusion.52, bf16[2048,1024]{1,0:T(8,128)(2,1)S(1)} %copy-done.5, s32[]{:T(128)S(6)} %select_n.8, bf16[2,256,1024]{2,1,0:T(8,128)(2,1)S(1)} %copy-done.9), kind=kOutput, calls=%fused_computation.18 | convolution fusion | flops 537133056 | bytes 4718596 | tf_op jit(solution)/shard_map/dot_general | solution.py:20
  122.8 2.7 %shard_map.129 = bf16[256,1024]{1,0:T(8,128)(2,1)} custom-call(f32[256,1024]{1,0:T(8,128)} %fusion.16.main_ref, f32[256,1024]{1,0:T(8,128)} %fusion.19.mirrored_ref), custom_call_target="tpu_custom_call" | custom-call | tf_op jit(solution)/shard_map/pallas_call | solution.py:373
  126.0 1.7 %fusion.25.mirrored_ref = f32[256,1024]{1,0:T(8,128)} fusion(f32[256,1024]{1,0:T(8,128)S(1)} %fusion.46, bf16[2048,1024]{1,0:T(8,128)(2,1)S(1)} %copy-done.5, s32[]{:T(128)S(6)} %select_n.11, bf16[2,256,1024]{2,1,0:T(8,128)(2,1)S(1)} %copy-done.9), kind=kOutput, calls=%fused_computation.21 | convolution fusion | flops 537133056 | bytes 4718596 | tf_op jit(solution)/shard_map/dot_general | solution.py:20
  127.8 1.7 %fusion.22.main_ref = f32[256,1024]{1,0:T(8,128)} fusion(f32[256,1024]{1,0:T(8,128)S(1)} %fusion.48, bf16[2048,1024]{1,0:T(8,128)(2,1)S(1)} %copy-done.5, s32[]{:T(128)S(6)} %select_n.10, bf16[2,256,1024]{2,1,0:T(8,128)(2,1)S(1)} %copy-done.9), kind=kOutput, calls=%fused_computation.20 | convolution fusion | flops 537133056 | bytes 4718596 | tf_op jit(solution)/shard_map/dot_general | solution.py:20
  130.5 1.7 %fusion.4.mirrored_ref = f32[256,1024]{1,0:T(8,128)} fusion(bf16[1024,2048]{1,0:T(8,128)(2,1)S(1)} %copy-done.7, s32[]{:T(128)S(6)} %select_n.11, bf16[2,256,1024]{2,1,0:T(8,128)(2,1)S(1)} %copy-done.11), kind=kOutput, calls=%fused_computation.4 | convolution fusion | flops 536870912 | bytes 3670020 | tf_op jit(solution)/shard_map/dot_general | solution.py:20
  132.2 2.8 %shard_map.131 = f32[256,1024]{1,0:T(8,128)} custom-call(f32[256,1024]{1,0:T(8,128)} %fusion.22.main_ref, f32[256,1024]{1,0:T(8,128)} %fusion.25.mirrored_ref), custom_call_target="tpu_custom_call" | custom-call | tf_op jit(solution)/shard_map/pallas_call | solution.py:373
  135.1 1.7 %fusion.6.main_ref = f32[256,1024]{1,0:T(8,128)} fusion(bf16[1024,2048]{1,0:T(8,128)(2,1)S(1)} %copy-done.8, s32[]{:T(128)S(6)} %select_n.10, bf16[2,256,1024]{2,1,0:T(8,128)(2,1)S(1)} %copy-done.11), kind=kOutput, calls=%fused_computation.6 | convolution fusion | flops 536870912 | bytes 3670020 | tf_op jit(solution)/shard_map/dot_general | solution.py:20
  136.7 2.9 %shard_map.130 = f32[256,1024]{1,0:T(8,128)} custom-call(f32[256,1024]{1,0:T(8,128)} %fusion.6.main_ref, f32[256,1024]{1,0:T(8,128)} %fusion.4.mirrored_ref), custom_call_target="tpu_custom_call" | custom-call | tf_op jit(solution)/shard_map/pallas_call | solution.py:373
  139.6 2.2 %add_convert_fusion.1 = bf16[256,1024]{1,0:T(8,128)(2,1)} fusion(f32[256,1024]{1,0:T(8,128)} %shard_map.130, bf16[256,1024]{1,0:T(8,128)(2,1)S(1)} %collective-permute-done), kind=kLoop, calls=%fused_computation.23 | loop fusion | flops 786432 | bytes 2097152 | tf_op jit(solution)/shard_map/convert_element_type | solution.py:488
  141.8 1.7 %collective-permute-done.1 = bf16[256,1024]{1,0:T(8,128)(2,1)S(1)} collective-permute-done((bf16[256,1024]{1,0:T(8,128)(2,1)S(1)}, bf16[256,1024]{1,0:T(8,128)(2,1)S(1)}, u32[]{:S(2)}, u32[]{:S(2)}) %collective-permute-start.1) | collective-permute-done | bytes 524320 | tf_op jit(solution)/shard_map/ppermute | solution.py:396
  143.5 0.9 add_convert_fusion
  (42 shorter events, 3.4 us)
Async XLA Ops:
  4.8 7.7 %copy-start.4 = (bf16[2048,1024]{1,0:T(8,128)(2,1)S(1)}, bf16[2048,1024]{1,0:T(8,128)(2,1)}, u32[]{:S(2)}) copy-start(bf16[2048,1024]{1,0:T(8,128)(2,1)} %param.13) | copy-start | bytes 12582916
  12.5 5.1 %copy-start.14 = (f32[8]{0:T(128)S(1)}, f32[8]{0:T(128)}, u32[]{:S(2)}) copy-start(f32[8]{0:T(128)} %param.18) | copy-start | bytes 100
  12.5 5.1 %copy-start.15 = (f32[8]{0:T(128)S(1)}, f32[8]{0:T(128)}, u32[]{:S(2)}) copy-start(f32[8]{0:T(128)} %param.17) | copy-start | bytes 100
  12.5 5.1 %copy-start.16 = (f32[8]{0:T(128)S(1)}, f32[8]{0:T(128)}, u32[]{:S(2)}) copy-start(f32[8]{0:T(128)} %param.16) | copy-start | bytes 100
  12.5 32.7 %copy-start.17 = (bf16[2,256,2048]{2,1,0:T(8,128)(2,1)S(1)}, bf16[2,256,2048]{2,1,0:T(8,128)(2,1)}, u32[]{:S(2)}) copy-start(bf16[2,256,2048]{2,1,0:T(8,128)(2,1)} %get-tuple-element.19) | copy-start | bytes 6291460
  21.7 1.0 copy-start
  44.4 0.7 copy-start.1
  45.1 20.3 %copy-start.6 = (bf16[1024,2048]{1,0:T(8,128)(2,1)S(1)}, bf16[1024,2048]{1,0:T(8,128)(2,1)}, u32[]{:S(2)}) copy-start(bf16[1024,2048]{1,0:T(8,128)(2,1)} %param.20) | copy-start | bytes 12582916
  65.4 2.8 %copy-start.11 = (bf16[2,256,1024]{2,1,0:T(8,128)(2,1)S(1)}, bf16[2,256,1024]{2,1,0:T(8,128)(2,1)}, u32[]{:S(2)}) copy-start(bf16[2,256,1024]{2,1,0:T(8,128)(2,1)} %get-tuple-element.29) | copy-start | bytes 3145732
  71.5 4.2 %copy-start.2 = (bf16[16,2,3,16,128]{4,3,2,1,0:T(8,128)(2,1)S(1)}, bf16[16,2,3,16,128]{4,3,2,1,0:T(8,128)(2,1)}, u32[]{:S(2)}) copy-start(bf16[16,2,3,16,128]{4,3,2,1,0:T(8,128)(2,1)} %get-tuple-element.23.parcel_ref) | copy-start | bytes 1179652
  74.2 42.7 %collective-permute-start = (bf16[256,1024]{1,0:T(8,128)(2,1)}, bf16[256,1024]{1,0:T(8,128)(2,1)S(1)}, u32[]{:S(2)}, u32[]{:S(2)}) collective-permute-start(bf16[256,1024]{1,0:T(8,128)(2,1)} %shard_map.126), channel_id=1, source_target_pairs={{0,1},{1,0},{2,3},{3,2},{4,5},{5,4},{6,7},{7,6},{8,9},{9,8},{10,11... | collective-permute-start | bytes 1572872 | tf_op jit(solution)/shard_map/ppermute | solution.py:396
  96.4 0.7 copy-start.3
  97.1 22.1 %copy-start.5 = (bf16[2048,1024]{1,0:T(8,128)(2,1)S(1)}, bf16[2048,1024]{1,0:T(8,128)(2,1)}, u32[]{:S(2)}) copy-start(bf16[2048,1024]{1,0:T(8,128)(2,1)} %param.13) | copy-start | bytes 12582916
  116.9 2.4 %copy-start.9 = (bf16[2,256,1024]{2,1,0:T(8,128)(2,1)S(1)}, bf16[2,256,1024]{2,1,0:T(8,128)(2,1)}, u32[]{:S(2)}) copy-start(bf16[2,256,1024]{2,1,0:T(8,128)(2,1)} %get-tuple-element.31) | copy-start | bytes 3145732
  122.8 2.7 %copy-start.13 = (bf16[2,256,128]{2,1,0:T(8,128)(2,1)S(1)}, bf16[2,256,128]{2,1,0:T(8,128)(2,1)}, u32[]{:S(2)}) copy-start(bf16[2,256,128]{2,1,0:T(8,128)(2,1)} %get-tuple-element.32) | copy-start | bytes 393220
  127.8 1.7 %copy-start.12 = (bf16[256,1024]{1,0:T(8,128)(2,1)S(1)}, bf16[256,1024]{1,0:T(8,128)(2,1)}, u32[]{:S(2)}) copy-start(bf16[256,1024]{1,0:T(8,128)(2,1)} %shard_map.129) | copy-start | bytes 1572868
  127.8 2.7 %copy-start.7 = (bf16[1024,2048]{1,0:T(8,128)(2,1)S(1)}, bf16[1024,2048]{1,0:T(8,128)(2,1)}, u32[]{:S(2)}) copy-start(bf16[1024,2048]{1,0:T(8,128)(2,1)} %param.20) | copy-start | bytes 12582916
  129.5 14.0 %collective-permute-start.1 = (bf16[256,1024]{1,0:T(8,128)(2,1)S(1)}, bf16[256,1024]{1,0:T(8,128)(2,1)S(1)}, u32[]{:S(2)}, u32[]{:S(2)}) collective-permute-start(bf16[256,1024]{1,0:T(8,128)(2,1)S(1)} %copy-done.12), channel_id=1, source_target_pairs={{0,1},{1,0},{2,3},{3,2},{4,5},{5,4},{6,7},{7,6},{8,9},{9,8},{10,11... | collective-permute-start | bytes 1572872 | tf_op jit(solution)/shard_map/ppermute | solution.py:396
  130.5 4.5 %copy-start.8 = (bf16[1024,2048]{1,0:T(8,128)(2,1)S(1)}, bf16[1024,2048]{1,0:T(8,128)(2,1)}, u32[]{:S(2)}) copy-start(bf16[1024,2048]{1,0:T(8,128)(2,1)} %param.20) | copy-start | bytes 12582916
  136.7 6.7 %copy-start.10 = (f32[256,1024]{1,0:T(8,128)S(1)}, f32[256,1024]{1,0:T(8,128)}, u32[]{:S(2)}) copy-start(f32[256,1024]{1,0:T(8,128)} %shard_map.131) | copy-start | bytes 3145732
where the time goes:
time: 145 us; the launch traced here: 144 us
  Pallas kernels  96 us (66%)
  matrix products  33.2 us (23%)
  local copies, waits for them, and re-layouts  6.73 us (5%)
  other arithmetic  4.03 us (3%)
  starting transfers between devices  2.03 us (1%)
  waiting for transfers between devices  1.68 us (1%)
    pallas_call x2, Pallas kernels, exchange(): pl.pallas_call(partial(exchange_kernel, upward), in_specs=[pl.BlockSpec(m...  42.4 us
    dot_general x15, matrix products, dot(): lax.dot_general(a, b, dims, preferred_element_type=f32, precision=precision)  33.2 us
    pallas_call x1, Pallas kernels, per_device(): pl.pallas_call(partial(grads_kernel, heads, state), grid=(2,), in_specs=[...  19.7 us
    pallas_call x1, Pallas kernels, per_device(): pl.pallas_call(partial(outputs_kernel, heads, state), grid=(2,), in_specs...  14.6 us
    pallas_call x4, Pallas kernels, merge(): pl.pallas_call(merge_kernel, out_shape=shape_of(dtype, *main.shape), comp...  11.1 us
    unnamed x38, local copies, waits for them, and re-layouts  5.17 us
    pallas_call x1, Pallas kernels, per_device(): pl.pallas_call(sources_kernel, out_shape=(shape_of(bf16, 2, length, width...  4.63 us
    pallas_call x1, Pallas kernels, per_device(): pl.pallas_call(partial(ends_kernel, heads, state), grid=(2,), in_specs=[b...  3.56 us
  transfers between devices with their start and end apart: 2, of which 1 were waited for; matrix products, arithmetic and copies ran while one was open for 4% of the time, Pallas kernels for 32%

commit v1 on v0

v1 whole, which is shorter than its diff:
```python
from functools import partial

import jax
import jax.numpy as jnp
from jax import lax
from jax.experimental import pallas as pl
from jax.experimental.pallas import tpu as pltpu
from jax.sharding import PartitionSpec as P

f32, bf16 = jnp.float32, jnp.bfloat16
epsilon = 1e-05
LANES = 128
CHUNK = 256
NN = (((1,), (0,)), ((), ()))
NT = (((1,), (1,)), ((), ()))
TN = (((0,), (0,)), ((), ()))
MESH_ID = pl.DeviceIdType.MESH
COLUMNS = ("cum", "exc", "low", "high", "grow_f", "grow_r", "tail_f", "tail_r")

NAMES = (
    "hidden_hbm", "cot_hbm", "wv_hbm", "wo_hbm", "ids", "step_t", "bc_t", "bias", "decay", "skip",
    "gain", "out", "dh", "src", "grd", "wv", "wo", "side", "x", "dz", "y", "z", "dy", "dx", "tail",
    "aux", "cols", "rows", "bc", "scores", "dscore", "bct", "keep", "end_row", "dec_row", "dec_got",
    "dec", "par", "got", "back", "fin", "out_snd", "out_rcv", "dh_snd", "dh_rcv", "load_sem",
    "dec_sem", "go_sem", "home_sem", "mp_sem", "barrier",
)

def dot(a, b, dims=NN):
    return lax.dot_general(a, b, dims, preferred_element_type=f32)


def iota2(shape, axis):
    return lax.broadcasted_iota(jnp.int32, shape, axis)


def mirror_matrix():
    return (iota2((CHUNK, CHUNK), 0) + iota2((CHUNK, CHUNK), 1) == CHUNK - 1).astype(bf16)


def chunk_at(start):
    return pl.ds(pl.multiple_of(start, CHUNK), CHUNK)


def lanes_of(h):
    return pl.ds(h * LANES, LANES)


def exact_dot(matrix, value, used):
    hi = value.astype(bf16).astype(f32)
    rest = value - hi
    mid = rest.astype(bf16).astype(f32)
    low = (rest - mid).astype(bf16).astype(f32)
    packed = hi + pltpu.roll(mid, used, 1) + pltpu.roll(low, 2 * used, 1)
    result = dot(matrix, packed.astype(bf16))
    result += pltpu.roll(result, LANES - used, 1) + pltpu.roll(result, LANES - 2 * used, 1)
    return jnp.where(iota2(value.shape, 1) < used, result, 0.0)


class Layer:
    def __init__(self, sizes, refs):
        self.length, self.width, self.inner, self.heads, self.state, self.count, self.parts = sizes
        for name, ref in zip(NAMES, refs):
            setattr(self, name, ref)
        self.me = lax.axis_index("seq")
        self.mine = lax.axis_index("mp")
        self.share = self.width // self.parts
        self.chunks = self.share // CHUNK

    def loads(self):
        top = self.src.at[pl.ds(0, self.length)]
        bottom = self.grd.at[pl.ds(0, self.length)]
        pairs = [(self.hidden_hbm, top), (self.wv_hbm, self.wv), (self.cot_hbm, bottom), (self.wo_hbm, self.wo)]
        return [pltpu.make_async_copy(a, b, self.load_sem.at[i]) for i, (a, b) in enumerate(pairs)]

    def peer(self, hop):
        return lax.rem(self.me + hop, self.count)

    def mp_peer(self, hop):
        return lax.rem(self.mine + hop, self.parts)

    def greet(self):
        def one(hop, none):
            pl.semaphore_signal(self.barrier, inc=1, device_id={"seq": self.peer(hop)}, device_id_type=MESH_ID)
            return none

        lax.fori_loop(1, self.count, one, 0)
        for hop in range(1, self.parts):
            pl.semaphore_signal(self.barrier, inc=1, device_id={"mp": self.mp_peer(hop)}, device_id_type=MESH_ID)

    def meet(self):
        pl.semaphore_wait(self.barrier, self.count + self.parts - 2)

    def decay_copy(self, hop):
        return pltpu.make_async_remote_copy(
            src_ref=self.dec_row, dst_ref=self.dec_got.at[self.me],
            send_sem=self.dec_sem.at[0, hop], recv_sem=self.dec_sem.at[1, hop],
            device_id={"seq": self.peer(hop)}, device_id_type=MESH_ID,
        )

    def go_copy(self, e, s, hop):
        k = 2 * e + s
        return pltpu.make_async_remote_copy(
            src_ref=self.par.at[e, s, self.peer(hop)], dst_ref=self.got.at[e, s, self.me],
            send_sem=self.go_sem.at[0, k, hop], recv_sem=self.go_sem.at[1, k, hop],
            device_id={"seq": self.peer(hop)}, device_id_type=MESH_ID,
        )

    def home_copy(self, e, s, hop):
        k = 2 * e + s
        return pltpu.make_async_remote_copy(
            src_ref=self.back.at[e, s, self.peer(hop)], dst_ref=self.fin.at[e, s, self.me],
            send_sem=self.home_sem.at[0, k, hop], recv_sem=self.home_sem.at[1, k, hop],
            device_id={"seq": self.peer(hop)}, device_id_type=MESH_ID,
        )

    def mp_copy(self, which, hop, k):
        snd, rcv = (self.out_snd, self.out_rcv) if which == 0 else (self.dh_snd, self.dh_rcv)
        return pltpu.make_async_remote_copy(
            src_ref=snd.at[hop - 1, k], dst_ref=rcv.at[hop - 1, k],
            send_sem=self.mp_sem.at[0, which, hop - 1, k], recv_sem=self.mp_sem.at[1, which, hop - 1, k],
            device_id={"mp": self.mp_peer(hop)}, device_id_type=MESH_ID,
        )

    def start(self, copy, *where):
        def one(hop, none):
            copy(*where, hop).start()
            return none

        lax.fori_loop(1, self.count, one, 0)

    def finish(self, copy, *where):
        def one(hop, none):
            copy(*where, hop).wait()
            return none

        lax.fori_loop(1, self.count, one, 0)

    def put_rows(self, ref, e, s, h, which, value):
        per, rows = self.count // self.heads, ref.shape[4]
        for k in range(per):
            ref[e, s, h * per + k, which] = value[k * rows : (k + 1) * rows].astype(bf16)

    def take_rows(self, ref, e, s, h, which):
        per = self.count // self.heads
        return jnp.concatenate([ref[e, s, h * per + k, which].astype(f32) for k in range(per)], axis=0)

    def scan(self, e, s):
        count, rows = self.count, self.got.shape[4]
        self.got[e, s, self.me] = self.par[e, s, self.me]
        zero = jnp.zeros((rows, LANES), f32)

        def step(i, totals):
            result = []
            for which in range(2):
                j = i if which == e else count - 1 - i
                self.back[e, s, j, which] = totals[which].astype(bf16)
                result.append(self.dec[s, pl.ds(j, 1)] * totals[which] + self.got[e, s, j, which].astype(f32))
            return tuple(result)

        lax.fori_loop(0, count, step, (zero, zero))

    def own_decays(self):
        count, heads = self.count, self.heads
        self.dec_got[self.me] = self.dec_row[...]
        table = jnp.concatenate([self.dec_got[j] for j in range(count)], axis=0)
        lane = iota2((count, LANES), 1)
        head = self.me // (count // heads)
        for s in range(2):
            picked = jnp.sum(jnp.where(lane == s * heads + head, table, 0.0), axis=1, keepdims=True)
            self.dec[s] = jnp.broadcast_to(picked, (count, LANES))

    def flip_into(self, ref):
        mirror = mirror_matrix()

        def one(k, none):
            tile = ref[pl.ds(0, self.length), chunk_at(k * CHUNK)]
            ref[pl.ds(self.length, self.length), chunk_at(self.width - CHUNK - k * CHUNK)] = dot(tile, mirror).astype(bf16)
            return none

        lax.fori_loop(0, self.width // CHUNK, one, 0)

    def side_weights(self):
        gap = LANES - self.heads - 2 * self.state
        self.side[...] = jnp.concatenate(
            [self.step_t[...].astype(f32), jnp.zeros((gap, self.width), f32), self.bc_t[...].astype(f32)], axis=0
        ).astype(bf16)

    def prepare(self):
        length, heads, state, used = self.length, self.heads, self.state, 2 * self.heads
        shape = (length, LANES)
        lane = iota2(shape, 1)
        aux = dot(self.src[...], self.side[...], NT)
        self.aux[0], self.aux[1] = aux[:length], aux[length:]
        raw = jnp.where(lane < heads, aux[:length], pltpu.roll(aux[length:], heads, 1))
        spare = jnp.zeros((1, LANES - used), f32)
        bias = jnp.concatenate([self.bias[...], self.bias[...], spare], axis=1)
        rate = jnp.exp(jnp.concatenate([self.decay[...], self.decay[...], spare], axis=1))
        shifted = jnp.where(lane < used, raw + bias, 0.0)
        dt = jnp.maximum(shifted, 0.0) + jnp.log1p(jnp.exp(-jnp.abs(shifted)))
        la = jnp.where(lane < used, -rate * dt, 0.0)
        lower = (iota2((length, length), 0) >= iota2((length, length), 1)).astype(bf16)
        cum = exact_dot(lower, la, used)
        exc = cum - la
        end = cum[length - 1 : length]
        log_dt = jnp.log(jnp.maximum(dt, 1e-38))
        grow_f, grow_r = jnp.exp(cum), jnp.exp(end - exc)
        tail_f, tail_r = dt * jnp.exp(end - cum), dt * jnp.exp(exc)
        values = (cum, exc, cum - log_dt, exc + log_dt, grow_f, grow_r, tail_f, tail_r)
        for i, value in enumerate(values):
            self.cols[i, 0] = value
            self.cols[i, 1] = pltpu.roll(value, LANES - heads, 1)
            flat = value.T
            self.rows[i, 0], self.rows[i, 1] = flat[:heads], flat[heads:used]
        sig = jax.nn.sigmoid(shifted)
        ratio = jnp.where(shifted < -15.0, 1.0, sig / jnp.maximum(dt, 1e-38))
        for i, value in ((0, sig * rate), (1, ratio)):
            self.keep[i, 0] = value
            self.keep[i, 1] = pltpu.roll(value, LANES - heads, 1)
        self.dec_row[...] = jnp.exp(end)
        for s in range(2):
            rounded = self.aux[s].astype(bf16)
            b_m, c_m = rounded[:, LANES - 2 * state : LANES - state], rounded[:, LANES - state :]
            self.bc[s, 0, :, :state] = b_m
            self.bc[s, 1, :, :state] = c_m
            self.bct[s] = rounded.astype(f32).T[LANES - 2 * state :]

    def row(self, name, s, h):
        return self.rows[COLUMNS.index(name), s, pl.ds(h, 1)]

    def col(self, name, s, h, at):
        return self.cols[COLUMNS.index(name), s, at, h : h + 1]

    def ends(self, s):
        b_t = self.bct[s, : self.state]
        for h in range(self.heads):
            left = jnp.concatenate([b_t * self.row("tail_f", s, h), b_t * self.row("tail_r", s, h)], axis=0).astype(bf16)
            both = dot(left, self.x[s, :, lanes_of(h)])
            self.put_rows(self.par, 0, s, h, 0, both[: self.state])
            self.put_rows(self.par, 0, s, h, 1, both[self.state :])

    def blocks(self):
        return [pl.ds(k * LANES, LANES) for k in range(self.length // LANES)]

    def local_outputs(self, s):
        at, state = self.blocks(), self.state
        b_m, c_m = self.bc[s, 0, :, :state], self.bc[s, 1, :, :state]
        self.scores[...] = dot(c_m, b_m, NT)
        below = iota2((LANES, LANES), 0) - iota2((LANES, LANES), 1)
        none = jnp.zeros((LANES, LANES), bf16)
        for h in range(self.heads):
            low_rows, high_rows = [], []
            for i, t in enumerate(at):
                cum, exc = self.col("cum", s, h, t), self.col("exc", s, h, t)
                low_cols, high_cols = [], []
                for j in range(len(at)):
                    cut = slice(j * LANES, (j + 1) * LANES)
                    to_f = lambda: cum - self.row("low", s, h)[:, cut]
                    to_r = lambda: self.row("high", s, h)[:, cut] - exc
                    power = to_f() if i > j else to_r() if i < j else jnp.minimum(to_f(), to_r())
                    mix = jnp.exp(power) * self.scores[t, cut]
                    low_cols.append(none if i < j else mix.astype(bf16) if i > j else jnp.where(below >= 0, mix, 0.0).astype(bf16))
                    high_cols.append(none if i > j else mix.astype(bf16) if i < j else jnp.where(below <= 0, mix, 0.0).astype(bf16))
                low_rows.append(jnp.concatenate(low_cols, axis=1))
                high_rows.append(jnp.concatenate(high_cols, axis=1))
            both = dot(jnp.concatenate(low_rows + high_rows, axis=0), self.x[s, :, lanes_of(h)])
            self.y[s, 0, :, lanes_of(h)] = both[: self.length]
            self.y[s, 1, :, lanes_of(h)] = both[self.length :]

    def finish_outputs(self, s):
        length, heads, state = self.length, self.heads, self.state
        at = self.blocks()
        c_m = self.bc[s, 1, :, :state]
        c_t = self.bct[s, state:]
        squares = [[jnp.zeros((LANES, LANES), f32) for _ in at] for _ in range(2)]
        for h in range(heads):
            for d, grow in ((0, "grow_f"), (1, "grow_r")):
                carried = dot(c_m, self.take_rows(self.fin, 0, s, h, d).astype(bf16))
                for i, t in enumerate(at):
                    y = self.y[s, d, t, lanes_of(h)] + self.col(grow, s, h, t) * carried[i * LANES : (i + 1) * LANES]
                    self.y[s, d, t, lanes_of(h)] = y
                    y += self.skip[:, h : h + 1] * self.x[s, t, lanes_of(h)].astype(f32)
                    squares[d][i] += y * y
        share = 1.0 / (heads * LANES)
        scale = [
            [lax.rsqrt(jnp.sum(q, axis=1, keepdims=True) * share + epsilon) for q in of_direction]
            for of_direction in squares
        ]
        means = []
        for i, t in enumerate(at):
            m_f, m_r = jnp.zeros((LANES, LANES), f32), jnp.zeros((LANES, LANES), f32)
            for h in range(heads):
                gain = self.gain[:, lanes_of(h)]
                direct = self.skip[:, h : h + 1] * self.x[s, t, lanes_of(h)].astype(f32)
                n_f = (self.y[s, 0, t, lanes_of(h)] + direct) * scale[0][i]
                n_r = (self.y[s, 1, t, lanes_of(h)] + direct) * scale[1][i]
                self.z[s, t, lanes_of(h)] = ((n_f + n_r) * gain).astype(bf16)
                g = self.dz[s, t, lanes_of(h)].astype(f32) * gain
                m_f += g * n_f
                m_r += g * n_r
            means.append([jnp.sum(m, axis=1, keepdims=True) * share for m in (m_f, m_r)])
        lane = iota2((LANES, LANES), 1)
        for i, t in enumerate(at):
            given = [jnp.zeros((LANES, LANES), f32) for _ in range(2)]
            pull = [scale[d][i] * scale[d][i] * means[i][d] for d in range(2)]
            for h in range(heads):
                g = self.dz[s, t, lanes_of(h)].astype(f32) * self.gain[:, lanes_of(h)]
                direct = self.skip[:, h : h + 1] * self.x[s, t, lanes_of(h)].astype(f32)
                for d in range(2):
                    y = self.y[s, d, t, lanes_of(h)]
                    grad = (scale[d][i] * g - pull[d] * (y + direct)).astype(bf16)
                    self.dy[s, d, t, lanes_of(h)] = grad
                    total = jnp.sum(grad.astype(f32) * y, axis=1, keepdims=True)
                    given[d] = jnp.where(lane == h, total, given[d])
            for d in range(2):
                self.cols[d, s, t] = given[d]
        for h in range(heads):
            for d, grow in ((0, "grow_f"), (1, "grow_r")):
                left = (c_t * self.row(grow, s, h)).astype(bf16)
                self.put_rows(self.par, 1, s, h, d, dot(left, self.dy[s, d, :, lanes_of(h)]))

    def local_grads(self, s):
        at, state = self.blocks(), self.state
        b_m, c_m = self.bc[s, 0, :, :state], self.bc[s, 1, :, :state]
        self.scores[...] = dot(b_m, c_m, NT)
        self.dscore[s] = jnp.zeros_like(self.scores)
        above = iota2((LANES, LANES), 1) - iota2((LANES, LANES), 0)
        none = jnp.zeros((LANES, LANES), bf16)
        for h in range(self.heads):
            x_h = self.x[s, :, lanes_of(h)]
            d_f, d_r = self.dy[s, 0, :, lanes_of(h)], self.dy[s, 1, :, lanes_of(h)]
            p_f, p_r = dot(x_h, d_f, NT), dot(x_h, d_r, NT)
            f_rows, r_rows = [], []
            for i, t in enumerate(at):
                low, high = self.col("low", s, h, t), self.col("high", s, h, t)
                f_cols, r_cols = [], []
                for j in range(len(at)):
                    here = slice(i * LANES, (i + 1) * LANES), slice(j * LANES, (j + 1) * LANES)
                    to_f = lambda: self.row("cum", s, h)[:, here[1]] - low
                    to_r = lambda: high - self.row("exc", s, h)[:, here[1]]
                    power = to_f() if i < j else to_r() if i > j else jnp.minimum(to_f(), to_r())
                    decay = jnp.exp(power)
                    weight = decay * self.scores[here]
                    if i < j:
                        picked = p_f[here]
                        f_cols.append(weight.astype(bf16))
                        r_cols.append(none)
                    elif i > j:
                        picked = p_r[here]
                        f_cols.append(none)
                        r_cols.append(weight.astype(bf16))
                    else:
                        picked = jnp.where(above >= 0, p_f[here], 0.0) + jnp.where(above <= 0, p_r[here], 0.0)
                        f_cols.append(jnp.where(above >= 0, weight, 0.0).astype(bf16))
                        r_cols.append(jnp.where(above <= 0, weight, 0.0).astype(bf16))
                    self.dscore[s, t, here[1]] += decay * picked
                f_rows.append(jnp.concatenate(f_cols, axis=1))
                r_rows.append(jnp.concatenate(r_cols, axis=1))
            self.y[s, 0, :, lanes_of(h)] = dot(jnp.concatenate(f_rows, axis=0), d_f)
            self.y[s, 1, :, lanes_of(h)] = dot(jnp.concatenate(r_rows, axis=0), d_r)

    def finish_grads(self, s):
        length, heads, state = self.length, self.heads, self.state
        at = self.blocks()
        b_m, c_m = self.bc[s, 0, :, :state], self.bc[s, 1, :, :state]
        lane = iota2((LANES, LANES), 1)
        lane_row = iota2((1, LANES), 1)
        zero = jnp.zeros((LANES, LANES), f32)
        into = [[zero for _ in at] for _ in range(2)]
        total = jnp.zeros((1, LANES), f32)
        d_b = jnp.zeros((length, state), f32)
        d_c = jnp.zeros((length, state), f32)
        ends = jnp.exp(self.end_row[s])
        for h in range(heads):
            x_h = self.x[s, :, lanes_of(h)]
            s_f, s_r = self.take_rows(self.fin, 0, s, h, 0), self.take_rows(self.fin, 0, s, h, 1)
            a_f, a_r = self.take_rows(self.fin, 1, s, h, 0), self.take_rows(self.fin, 1, s, h, 1)
            own, own_r = self.take_rows(self.par, 0, s, h, 0), self.take_rows(self.par, 1, s, h, 1)
            whole = pl.ds(0, length)
            tail_f, tail_r = self.col("tail_f", s, h, whole), self.col("tail_r", s, h, whole)
            u_f, u_r = dot(b_m, a_f.astype(bf16)), dot(b_m, a_r.astype(bf16))
            d_b += dot(x_h, a_f.astype(bf16), NT) * tail_f + dot(x_h, a_r.astype(bf16), NT) * tail_r
            d_c += dot(self.dy[s, 0, :, lanes_of(h)], s_f.astype(bf16), NT) * self.col("grow_f", s, h, whole)
            d_c += dot(self.dy[s, 1, :, lanes_of(h)], s_r.astype(bf16), NT) * self.col("grow_r", s, h, whole)
            for i, t in enumerate(at):
                cut = slice(i * LANES, (i + 1) * LANES)
                x = self.x[s, t, lanes_of(h)].astype(f32)
                u = [
                    self.y[s, 0, t, lanes_of(h)] + tail_f[cut] * u_f[cut],
                    self.y[s, 1, t, lanes_of(h)] + tail_r[cut] * u_r[cut],
                ]
                skipped = self.dy[s, 0, t, lanes_of(h)].astype(f32) + self.dy[s, 1, t, lanes_of(h)].astype(f32)
                self.dx[s, t, lanes_of(h)] = (u[0] + u[1] + self.skip[:, h : h + 1] * skipped).astype(bf16)
                for d in range(2):
                    into[d][i] = jnp.where(lane == h, jnp.sum(x * u[d], axis=1, keepdims=True), into[d][i])
            decay = ends[:, h : h + 1]
            ending = a_f * (decay * s_f + own) + s_r * (decay * a_r + own_r)
            ended = jnp.sum(jnp.sum(ending, axis=0, keepdims=True), axis=1, keepdims=True)
            total = jnp.where(lane_row == h, ended, total)
        into_f, into_r = (jnp.concatenate(rows, axis=0) for rows in into)
        d_cum = self.cols[0, s] - into_f
        d_exc = into_r - self.cols[1, s]
        upper = (iota2((length, length), 0) <= iota2((length, length), 1)).astype(bf16)
        d_la = exact_dot(upper, d_cum + d_exc, heads) - d_exc + total
        d_raw = (into_f + into_r) * self.keep[1, s] - self.keep[0, s] * d_la
        d_raw = jnp.where(iota2((length, LANES), 1) < heads, d_raw, 0.0)
        scores = self.dscore[s].astype(bf16)
        d_b += dot(scores, c_m)
        d_c += dot(scores, b_m, TN)
        self.tail[s] = jnp.concatenate([d_raw[:, : LANES - 2 * state], d_b, d_c], axis=1).astype(bf16)

    def out_chunk(self, part, k):
        first = part * self.share + k * CHUNK
        there = self.width - CHUNK - first
        mirrored = dot(self.z[1], self.wo[:, chunk_at(there)]).astype(bf16)
        return dot(self.z[0], self.wo[:, chunk_at(first)]) + dot(mirrored, mirror_matrix())

    def hidden_chunk(self, part, k):
        first = part * self.share + k * CHUNK
        there = self.width - CHUNK - first

        def term(s, at):
            return dot(self.dx[s], self.wv[chunk_at(at), :], NT) + dot(self.tail[s], self.side[:, chunk_at(at)])

        return term(0, first) + dot(term(1, there).astype(bf16), mirror_matrix())

    def send_parts(self, which, chunk):
        snd = self.out_snd if which == 0 else self.dh_snd
        for hop in range(1, self.parts):

            def one(k, none, hop=hop):
                snd[hop - 1, k] = chunk(self.mp_peer(hop), k).astype(bf16)
                self.mp_copy(which, hop, k).start()
                return none

            lax.fori_loop(0, self.chunks, one, 0)

    def own_part(self, which, chunk):
        rcv, out = (self.out_rcv, self.out) if which == 0 else (self.dh_rcv, self.dh)

        def one(k, none):
            value = chunk(self.mine, k)
            for hop in range(1, self.parts):
                self.mp_copy(which, hop, k).wait()
                value += rcv[hop - 1, k].astype(f32)
            out[:, chunk_at(k * CHUNK)] = value.astype(bf16)
            return none

        lax.fori_loop(0, self.chunks, one, 0)


def each_stream(body):
    def one(s, none):
        body(s)
        return none

    lax.fori_loop(0, 2, one, 0)


def layer_kernel(sizes, *refs):
    layer = Layer(sizes, refs + (pltpu.get_barrier_semaphore(),))
    length, inner = layer.length, layer.inner
    hidden_load, value_load, cot_load, out_load = layer.loads()
    for load in (hidden_load, value_load, cot_load, out_load):
        load.start()
    layer.greet()
    layer.side_weights()
    hidden_load.wait()
    layer.flip_into(layer.src)
    layer.prepare()
    for s in range(2):
        layer.end_row[s] = layer.cols[0, s, length - 1 : length]
    layer.meet()
    layer.start(layer.decay_copy)
    value_load.wait()

    def values(k, none):
        at = chunk_at(k * CHUNK)
        both = dot(layer.src[...], layer.wv[:, at]).astype(bf16)
        layer.x[0, :, at], layer.x[1, :, at] = both[:length], both[length:]
        return none

    lax.fori_loop(0, inner // CHUNK, values, 0)

    def leave(s):
        layer.ends(s)
        layer.start(layer.go_copy, 0, s)

    each_stream(leave)
    cot_load.wait()
    layer.flip_into(layer.grd)
    known = jnp.where(layer.ids[...] != 4, 1.0, 0.0)
    known = jnp.broadcast_to(known, (8, length)).T[:, :1] > 0.5
    out_load.wait()

    def output_grads(k, none):
        at = chunk_at(k * CHUNK)
        both = dot(layer.grd[...], layer.wo[at, :], NT)
        layer.dz[0, :, at] = jnp.where(known, both[:length], 0.0).astype(bf16)
        layer.dz[1, :, at] = jnp.where(known, both[length:], 0.0).astype(bf16)
        return none

    lax.fori_loop(0, inner // CHUNK, output_grads, 0)
    layer.finish(layer.decay_copy)
    layer.own_decays()

    def turn(e, work, s):
        layer.finish(layer.go_copy, e, s)
        layer.scan(e, s)
        layer.start(layer.home_copy, e, s)
        work(s)

    def arrive(e, s):
        layer.finish(layer.home_copy, e, s)
        layer.fin[e, s, layer.me] = layer.back[e, s, layer.me]

    each_stream(partial(turn, 0, layer.local_outputs))

    def outputs(s):
        arrive(0, s)
        layer.finish_outputs(s)
        layer.start(layer.go_copy, 1, s)

    each_stream(outputs)
    layer.send_parts(0, layer.out_chunk)
    each_stream(partial(turn, 1, layer.local_grads))

    def gradients(s):
        arrive(1, s)
        layer.finish_grads(s)

    each_stream(gradients)
    layer.send_parts(1, layer.hidden_chunk)
    layer.own_part(0, layer.out_chunk)
    layer.own_part(1, layer.hidden_chunk)


def per_device(
    hidden, ids, w_value, w_bc, w_step, step_bias, decay_log, skip, norm_gain, w_out, cotangent
):
    length, width = hidden.shape
    heads, inner, state = w_step.shape[1], w_value.shape[1], w_bc.shape[2] // 2
    count, parts = lax.axis_size("seq"), lax.axis_size("mp")
    assert w_bc.shape[1] == 1 and inner == heads * LANES
    assert count % heads == 0 and (heads * state) % count == 0
    rows = heads * state // count
    share = width // parts
    chunks = share // CHUNK
    vmem, anywhere = pl.BlockSpec(memory_space=pltpu.VMEM), pl.BlockSpec(memory_space=pl.ANY)
    parcel = (2, 2, count, 2, rows, LANES)
    travel = (max(parts - 1, 1), chunks, length, CHUNK)
    sem = pltpu.SemaphoreType.DMA
    scratch = [
        pltpu.VMEM((2 * length, width), bf16),
        pltpu.VMEM((2 * length, width), bf16),
        pltpu.VMEM(w_value.shape, bf16),
        pltpu.VMEM(w_out.shape, bf16),
        pltpu.VMEM((LANES, width), bf16),
        pltpu.VMEM((2, length, inner), bf16),
        pltpu.VMEM((2, length, inner), bf16),
        pltpu.VMEM((2, 2, length, inner), f32),
        pltpu.VMEM((2, length, inner), bf16),
        pltpu.VMEM((2, 2, length, inner), bf16),
        pltpu.VMEM((2, length, inner), bf16),
        pltpu.VMEM((2, length, LANES), bf16),
        pltpu.VMEM((2, length, LANES), f32),
        pltpu.VMEM((len(COLUMNS), 2, length, LANES), f32),
        pltpu.VMEM((len(COLUMNS), 2, heads, length), f32),
        pltpu.VMEM((2, 2, length, LANES), bf16),
        pltpu.VMEM((length, length), f32),
        pltpu.VMEM((2, length, length), f32),
        pltpu.VMEM((2, 2 * state, length), f32),
        pltpu.VMEM((2, 2, length, LANES), f32),
        pltpu.VMEM((2, 1, LANES), f32),
        pltpu.VMEM((1, LANES), f32),
        pltpu.VMEM((count, 1, LANES), f32),
        pltpu.VMEM((2, count, LANES), f32),
        pltpu.VMEM(parcel, bf16),
        pltpu.VMEM(parcel, bf16),
        pltpu.VMEM(parcel, bf16),
        pltpu.VMEM(parcel, bf16),
        pltpu.VMEM(travel, bf16),
        pltpu.VMEM(travel, bf16),
        pltpu.VMEM(travel, bf16),
        pltpu.VMEM(travel, bf16),
        sem((4,)),
        sem((2, count)),
        sem((2, 4, count)),
        sem((2, 4, count)),
        sem((2, 2, max(parts - 1, 1), chunks)),
    ]
    sizes = (length, width, inner, heads, state, count, parts)
    return pl.pallas_call(
        partial(layer_kernel, sizes),
        in_specs=[anywhere] * 4 + [vmem] * 7,
        out_specs=(vmem, vmem),
        out_shape=(jax.ShapeDtypeStruct((length, share), bf16),) * 2,
        scratch_shapes=scratch,
        compiler_params=pltpu.CompilerParams(
            collective_id=0, has_side_effects=True, vmem_limit_bytes=56 * 1024 * 1024
        ),
    )(
        hidden, cotangent, w_value, w_out, ids[None], w_step.T, w_bc.reshape(width, -1).T,
        step_bias[None], decay_log[None], skip[None], norm_gain[None],
    )


def solution(mesh):
    in_specs = (
        P("seq", None),
        P("seq"),
        P(None, "mp"),
        P(None, "mp", None),
        P(None, "mp"),
        P("mp"),
        P("mp"),
        P("mp"),
        P("mp"),
        P("mp", None),
        P("seq", None),
    )
    out_specs = (P("seq", "mp"), P("seq", "mp"))
    return jax.shard_map(
        per_device, mesh=mesh, in_specs=in_specs, out_specs=out_specs, check_vma=False
    )
```

time: 145 us -> 71.3 us (0.49)
  matrix products: 33.2 us -> 0 us
  Pallas kernels: 96 us -> 66.7 us
  other arithmetic: 4.03 us -> 0 us
  local copies, waits for them, and re-layouts: 6.73 us -> 3.74 us
  starting transfers between devices: 2.03 us -> 0 us
  waiting for transfers between devices: 1.68 us -> 0 us
    dot_general x15 -> x0, matrix products: 33.2 us -> none  [dot(): lax.dot_general(a, b, dims, preferred_element_type=f32, precision=precision)]
    pallas_call x10 -> x1, Pallas kernels: 96 us -> 66.7 us  [per_device(): pl.pallas_call(partial(layer_kernel, sizes), in_specs=[anywhere] * 4 + [v...]
    convert_element_type x2 -> x0, other arithmetic: 3.1 us -> none  [per_device(): return (out.astype(bf16), d_hidden.astype(bf16))]
    ppermute x2 -> x0, starting transfers between devices: 2.03 us -> none  [send_on(): lax.ppermute(leaving, 'mp', [(i, (i + hop) % parts) for i in range(parts)])]
    ppermute x2 -> x0, waiting for transfers between devices: 1.68 us -> none  [send_on(): lax.ppermute(leaving, 'mp', [(i, (i + hop) % parts) for i in range(parts)])]
    broadcast_in_dim x2 -> x0, local copies, waits for them, and re-layouts: 1.48 us -> none  [the longest x1 1.48 us: per_device(): ids[:, None]]
    unnamed x38 -> x2, local copies, waits for them, and re-layouts: 5.17 us -> 3.74 us
  transfers between devices with their start and end apart: 2 -> 0, of which waited for: 1 -> 0; matrix products, arithmetic and copies ran while one was open for 4% -> 0% of each run, Pallas kernels for 32% -> 0%
where the time goes in v1:
time: 71.3 us; the launch traced here: 71.1 us
  Pallas kernels  66.7 us (94%)
  local copies, waits for them, and re-layouts  3.74 us (5%)
    pallas_call x1, Pallas kernels, per_device(): pl.pallas_call(partial(layer_kernel, sizes), in_specs=[anywhere] * 4 + [v...  66.7 us
    unnamed x2, local copies, waits for them, and re-layouts  3.74 us

profile of v1, /device:TPU:0, one launch (start us, length us, event | category | flops | bytes accessed | tf_op | source)
XLA Modules:
  0.0 71.1 jit_solution(15991131430078063447)
XLA Ops:
  0.6 66.7 %shard_map.122 = (bf16[256,1024]{1,0:T(8,128)(2,1)}, bf16[256,1024]{1,0:T(8,128)(2,1)}) custom-call(bf16[256,2048]{1,0:T(8,128)(2,1)} %refs_0_.1, bf16[256,2048]{1,0:T(8,128)(2,1)} %refs_1_.1, bf16[2048,1024]{1,0:T(8,128)(2,1)} %refs_2_.1, bf16[1024,2048]{1,0:T(8,128)(2,1)} %refs_3_.1, s32[1,256]{1,0:T(1,128)} %bitcast.12, bf16[8,2048]{1,0:T(8,128)(2,1)} %bitcast.10, ...), custom_call_target="tpu_custom_call" | custom-call | tf_op jit(solution)/shard_map/pallas_call | solution.py:592
  67.4 1.9 %copy.15 = bf16[256,1024]{1,0:T(8,128)(2,1)} copy(bf16[256,1024]{1,0:T(8,128)(2,1)} %get-tuple-element.4) | data formatting | bytes 1048576
  69.2 1.9 %copy.16 = bf16[256,1024]{1,0:T(8,128)(2,1)} copy(bf16[256,1024]{1,0:T(8,128)(2,1)} %get-tuple-element.5) | data formatting | bytes 1048576

commit v2 on v1

v2 whole, which is shorter than its diff:
```python
from functools import partial

import jax
import jax.numpy as jnp
from jax import lax
from jax.experimental import pallas as pl
from jax.experimental.pallas import tpu as pltpu
from jax.sharding import PartitionSpec as P

f32, bf16 = jnp.float32, jnp.bfloat16
epsilon = 1e-05
LANES = 128
CHUNK = 256
NN = (((1,), (0,)), ((), ()))
NT = (((1,), (1,)), ((), ()))
TN = (((0,), (0,)), ((), ()))
MESH_ID = pl.DeviceIdType.MESH
COLUMNS = ("cum", "exc", "low", "high", "grow_f", "grow_r", "tail_f", "tail_r")

NAMES = (
    "hidden_hbm", "cot_hbm", "wv_hbm", "wo_hbm", "ids", "step_t", "bc_t", "bias", "decay", "skip",
    "gain", "out", "dh", "src", "grd", "wv", "wo", "side", "x", "dz", "y", "z", "dy", "dx", "tail",
    "aux", "cols", "rows", "bc", "scores", "dscore", "carried", "bct", "keep", "end_row", "dec_row",
    "dec_got", "dec", "plane_dec", "par", "got", "agg", "far", "back", "fin", "out_snd", "out_rcv",
    "dh_snd", "dh_rcv", "hold", "load_sem", "dec_sem", "go_sem", "far_sem", "home_sem", "mp_sem",
    "barrier",
)


def dot(a, b, dims=NN):
    return lax.dot_general(a, b, dims, preferred_element_type=f32)


def iota2(shape, axis):
    return lax.broadcasted_iota(jnp.int32, shape, axis)


def mirror_matrix():
    return (iota2((CHUNK, CHUNK), 0) + iota2((CHUNK, CHUNK), 1) == CHUNK - 1).astype(bf16)


def chunk_at(start):
    return pl.ds(pl.multiple_of(start, CHUNK), CHUNK)


def lanes_of(h):
    return pl.ds(h * LANES, LANES)


def exact_dot(matrix, value, used):
    hi = value.astype(bf16).astype(f32)
    rest = value - hi
    mid = rest.astype(bf16).astype(f32)
    low = (rest - mid).astype(bf16).astype(f32)
    packed = hi + pltpu.roll(mid, used, 1) + pltpu.roll(low, 2 * used, 1)
    result = dot(matrix, packed.astype(bf16))
    result += pltpu.roll(result, LANES - used, 1) + pltpu.roll(result, LANES - 2 * used, 1)
    return jnp.where(iota2(value.shape, 1) < used, result, 0.0)


class Layer:
    def __init__(self, sizes, refs):
        self.length, self.width, self.inner, self.heads, self.state, self.count, self.group, self.parts = sizes
        for name, ref in zip(NAMES, refs):
            setattr(self, name, ref)
        self.planes = self.count // self.group
        self.each = self.heads // self.group
        me = lax.axis_index("seq")
        self.me, self.plane, self.member = me, me // self.group, lax.rem(me, self.group)
        self.mine = lax.axis_index("mp")
        self.share = self.width // self.parts
        self.chunks = self.share // CHUNK

    def loads(self):
        top = self.src.at[pl.ds(0, self.length)]
        bottom = self.grd.at[pl.ds(0, self.length)]
        pairs = [(self.hidden_hbm, top), (self.wv_hbm, self.wv), (self.cot_hbm, bottom), (self.wo_hbm, self.wo)]
        return [pltpu.make_async_copy(a, b, self.load_sem.at[i]) for i, (a, b) in enumerate(pairs)]

    def peer(self, hop):
        return lax.rem(self.me + hop, self.count)

    def greet(self):
        def one(hop, none):
            pl.semaphore_signal(self.barrier, inc=1, device_id={"seq": self.peer(hop)}, device_id_type=MESH_ID)
            return none

        lax.fori_loop(1, self.count, one, 0)
        pl.semaphore_signal(self.barrier, inc=1, device_id={"mp": 1 - self.mine}, device_id_type=MESH_ID)

    def meet(self):
        pl.semaphore_wait(self.barrier, self.count)

    def remote(self, src, dst, sems, where, device):
        return pltpu.make_async_remote_copy(
            src_ref=src, dst_ref=dst, send_sem=sems.at[(0,) + where], recv_sem=sems.at[(1,) + where],
            device_id=device, device_id_type=MESH_ID,
        )

    def decay_copy(self, hop):
        return self.remote(self.dec_row, self.dec_got.at[self.me], self.dec_sem, (hop,), {"seq": self.peer(hop)})

    def start_decays(self):
        def one(hop, none):
            self.decay_copy(hop).start()
            return none

        lax.fori_loop(1, self.count, one, 0)

    def finish_decays(self):
        def one(hop, none):
            self.decay_copy(hop).wait()
            return none

        lax.fori_loop(1, self.count, one, 0)

    def gather_copies(self, e, s):
        for hop in range(1, self.group):
            to = lax.rem(self.member + hop, self.group)
            yield self.remote(
                self.par.at[e, s, to], self.got.at[e, s, self.member], self.go_sem, (2 * e + s, hop),
                {"seq": self.plane * self.group + to},
            )

    def plane_copies(self, e, s):
        for hop in range(1, self.planes):
            to = lax.rem(self.plane + hop, self.planes)
            which = jnp.where(to > self.plane, e, 1 - e)
            yield self.remote(
                self.agg.at[e, s, which], self.far.at[e, s, self.plane], self.far_sem, (2 * e + s, hop),
                {"seq": to * self.group + self.member},
            )

    def home_copies(self, e, s):
        for hop in range(1, self.group):
            to = lax.rem(self.member + hop, self.group)
            yield self.remote(
                self.back.at[e, s, to], self.fin.at[e, s, self.member], self.home_sem, (2 * e + s, hop),
                {"seq": self.plane * self.group + to},
            )

    def mp_copy(self, which, k):
        snd, rcv = (self.out_snd, self.out_rcv) if which == 0 else (self.dh_snd, self.dh_rcv)
        return self.remote(snd.at[k], rcv.at[k], self.mp_sem, (which, k), {"mp": 1 - self.mine})

    def put_rows(self, e, s, h, which, value):
        at = pl.ds(h % self.each * self.state, self.state)
        self.par[e, s, h // self.each, which, at] = value.astype(bf16)

    def take_rows(self, ref, e, s, h, which):
        return ref[e, s, h // self.each, which, pl.ds(h % self.each * self.state, self.state)]

    def own_decays(self):
        self.dec_got[self.me] = self.dec_row[...]
        table = jnp.concatenate([self.dec_got[j] for j in range(self.count)], axis=0)
        lane = iota2((self.count, LANES), 1)
        for s in range(2):
            for q in range(self.each):
                head = s * self.heads + self.member * self.each + q
                picked = jnp.sum(jnp.where(lane == head, table, 0.0), axis=1, keepdims=True)
                wide = jnp.broadcast_to(picked, (self.count, LANES))
                self.dec[s, q] = wide
                for p in range(self.planes):
                    product = wide[p * self.group : p * self.group + 1]
                    for m in range(1, self.group):
                        product = product * wide[p * self.group + m : p * self.group + m + 1]
                    self.plane_dec[s, q, p : p + 1] = product

    def members(self, e, s, which, q, total, visit):
        order = range(self.group) if which == e else range(self.group - 1, -1, -1)
        at = pl.ds(q * self.state, self.state)
        for m in order:
            visit(m, at, total)
            decay = self.dec[s, q, pl.ds(self.plane * self.group + m, 1)]
            total = decay * total + self.got[e, s, m, which, at].astype(f32)
        return total

    def begin(self, e, s):
        for copy in self.gather_copies(e, s):
            copy.start()

    def spread(self, e, s):
        for copy in self.gather_copies(e, s):
            copy.wait()
        self.got[e, s, self.member] = self.par[e, s, self.member]
        self.far[e, s, self.plane] = jnp.zeros((self.each * self.state, LANES), bf16)
        for which in range(2):
            for q in range(self.each):
                total = self.members(e, s, which, q, jnp.zeros((self.state, LANES), f32), lambda m, at, total: None)
                self.agg[e, s, which, pl.ds(q * self.state, self.state)] = total.astype(bf16)
        for copy in self.plane_copies(e, s):
            copy.start()

    def send_home(self, e, s):
        for copy in self.plane_copies(e, s):
            copy.wait()
        for which in range(2):
            rising = which == e
            for q in range(self.each):
                total = jnp.zeros((self.state, LANES), f32)
                for p in range(self.planes) if rising else range(self.planes - 1, -1, -1):
                    got = self.far[e, s, p, pl.ds(q * self.state, self.state)].astype(f32)
                    longer = self.plane_dec[s, q, p : p + 1] * total + got
                    total = jnp.where(p < self.plane if rising else p > self.plane, longer, total)

                def keep(m, at, value):
                    self.back[e, s, m, which, at] = value.astype(bf16)

                self.members(e, s, which, q, total, keep)
        for copy in self.home_copies(e, s):
            copy.start()

    def arrive(self, e, s):
        for copy in self.home_copies(e, s):
            copy.wait()
        self.fin[e, s, self.member] = self.back[e, s, self.member]

    def flip_into(self, ref):
        mirror = mirror_matrix()
        for k in range(self.width // CHUNK):
            tile = ref[pl.ds(0, self.length), pl.ds(k * CHUNK, CHUNK)]
            there = pl.ds(self.width - CHUNK - k * CHUNK, CHUNK)
            ref[pl.ds(self.length, self.length), there] = dot(tile, mirror).astype(bf16)

    def side_weights(self):
        gap = LANES - self.heads - 2 * self.state
        self.side[...] = jnp.concatenate(
            [self.step_t[...].astype(f32), jnp.zeros((gap, self.width), f32), self.bc_t[...].astype(f32)], axis=0
        ).astype(bf16)

    def prepare(self):
        length, heads, state, used = self.length, self.heads, self.state, 2 * self.heads
        shape = (length, LANES)
        lane = iota2(shape, 1)
        aux = dot(self.src[...], self.side[...], NT)
        self.aux[0], self.aux[1] = aux[:length], aux[length:]
        raw = jnp.where(lane < heads, aux[:length], pltpu.roll(aux[length:], heads, 1))
        spare = jnp.zeros((1, LANES - used), f32)
        bias = jnp.concatenate([self.bias[...], self.bias[...], spare], axis=1)
        rate = jnp.exp(jnp.concatenate([self.decay[...], self.decay[...], spare], axis=1))
        shifted = jnp.where(lane < used, raw + bias, 0.0)
        dt = jnp.maximum(shifted, 0.0) + jnp.log1p(jnp.exp(-jnp.abs(shifted)))
        la = jnp.where(lane < used, -rate * dt, 0.0)
        lower = (iota2((length, length), 0) >= iota2((length, length), 1)).astype(bf16)
        cum = exact_dot(lower, la, used)
        exc = cum - la
        end = cum[length - 1 : length]
        log_dt = jnp.log(jnp.maximum(dt, 1e-38))
        grow_f, grow_r = jnp.exp(cum), jnp.exp(end - exc)
        tail_f, tail_r = dt * jnp.exp(end - cum), dt * jnp.exp(exc)
        values = (cum, exc, cum - log_dt, exc + log_dt, grow_f, grow_r, tail_f, tail_r)
        for i, value in enumerate(values):
            self.cols[i, 0] = value
            self.cols[i, 1] = pltpu.roll(value, LANES - heads, 1)
            flat = value.T
            self.rows[i, 0], self.rows[i, 1] = flat[:heads], flat[heads:used]
        sig = jax.nn.sigmoid(shifted)
        ratio = jnp.where(shifted < -15.0, 1.0, sig / jnp.maximum(dt, 1e-38))
        for i, value in ((0, sig * rate), (1, ratio)):
            self.keep[i, 0] = value
            self.keep[i, 1] = pltpu.roll(value, LANES - heads, 1)
        self.dec_row[...] = jnp.exp(end)
        for s in range(2):
            rounded = self.aux[s].astype(bf16)
            b_m, c_m = rounded[:, LANES - 2 * state : LANES - state], rounded[:, LANES - state :]
            self.bc[s, 0, :, :state] = b_m
            self.bc[s, 1, :, :state] = c_m
            self.bct[s] = rounded.astype(f32).T[LANES - 2 * state :]

    def row(self, name, s, h):
        return self.rows[COLUMNS.index(name), s, pl.ds(h, 1)]

    def col(self, name, s, h, at):
        return self.cols[COLUMNS.index(name), s, at, h : h + 1]

    def ends(self, s):
        b_t = self.bct[s, : self.state]
        for h in range(self.heads):
            left = jnp.concatenate([b_t * self.row("tail_f", s, h), b_t * self.row("tail_r", s, h)], axis=0).astype(bf16)
            both = dot(left, self.x[s, :, lanes_of(h)])
            self.put_rows(0, s, h, 0, both[: self.state])
            self.put_rows(0, s, h, 1, both[self.state :])

    def blocks(self):
        return [pl.ds(k * LANES, LANES) for k in range(self.length // LANES)]

    def local_outputs(self, s):
        at, state = self.blocks(), self.state
        b_m, c_m = self.bc[s, 0, :, :state], self.bc[s, 1, :, :state]
        self.scores[...] = dot(c_m, b_m, NT)
        below = iota2((LANES, LANES), 0) - iota2((LANES, LANES), 1)
        none = jnp.zeros((LANES, LANES), bf16)
        for h in range(self.heads):
            low_rows, high_rows = [], []
            for i, t in enumerate(at):
                cum, exc = self.col("cum", s, h, t), self.col("exc", s, h, t)
                low_cols, high_cols = [], []
                for j in range(len(at)):
                    cut = slice(j * LANES, (j + 1) * LANES)
                    to_f = lambda: cum - self.row("low", s, h)[:, cut]
                    to_r = lambda: self.row("high", s, h)[:, cut] - exc
                    power = to_f() if i > j else to_r() if i < j else jnp.minimum(to_f(), to_r())
                    mix = jnp.exp(power) * self.scores[t, cut]
                    low_cols.append(none if i < j else mix.astype(bf16) if i > j else jnp.where(below >= 0, mix, 0.0).astype(bf16))
                    high_cols.append(none if i > j else mix.astype(bf16) if i < j else jnp.where(below <= 0, mix, 0.0).astype(bf16))
                low_rows.append(jnp.concatenate(low_cols, axis=1))
                high_rows.append(jnp.concatenate(high_cols, axis=1))
            both = dot(jnp.concatenate(low_rows + high_rows, axis=0), self.x[s, :, lanes_of(h)])
            self.y[s, 0, :, lanes_of(h)] = both[: self.length]
            self.y[s, 1, :, lanes_of(h)] = both[self.length :]

    def finish_outputs(self, s):
        length, heads, state = self.length, self.heads, self.state
        at = self.blocks()
        c_m = self.bc[s, 1, :, :state]
        c_t = self.bct[s, state:]
        zero = jnp.zeros((LANES, LANES), f32)
        squares = [[zero for _ in at] for _ in range(2)]
        pulls = [[zero for _ in at] for _ in range(2)]
        for h in range(heads):
            carried = [dot(c_m, self.take_rows(self.fin, 0, s, h, d)) for d in range(2)]
            for i, t in enumerate(at):
                g = self.dz[s, t, lanes_of(h)].astype(f32) * self.gain[:, lanes_of(h)]
                direct = self.skip[:, h : h + 1] * self.x[s, t, lanes_of(h)].astype(f32)
                for d, grow in ((0, "grow_f"), (1, "grow_r")):
                    y = self.y[s, d, t, lanes_of(h)] + self.col(grow, s, h, t) * carried[d][i * LANES : (i + 1) * LANES]
                    y += direct
                    self.y[s, d, t, lanes_of(h)] = y
                    squares[d][i] += y * y
                    pulls[d][i] += g * y
        share = 1.0 / (heads * LANES)
        lane = iota2((LANES, LANES), 1)
        for i, t in enumerate(at):
            scale = [lax.rsqrt(jnp.sum(squares[d][i], axis=1, keepdims=True) * share + epsilon) for d in range(2)]
            means = [scale[d] * jnp.sum(pulls[d][i], axis=1, keepdims=True) * share for d in range(2)]
            pull = [scale[d] * scale[d] * means[d] for d in range(2)]
            given = [zero, zero]
            for h in range(heads):
                gain = self.gain[:, lanes_of(h)]
                g = self.dz[s, t, lanes_of(h)].astype(f32) * gain
                direct = self.skip[:, h : h + 1] * self.x[s, t, lanes_of(h)].astype(f32)
                y = [self.y[s, d, t, lanes_of(h)] for d in range(2)]
                rows = pl.ds(s * length + i * LANES, LANES)
                self.z[rows, lanes_of(h)] = ((y[0] * scale[0] + y[1] * scale[1]) * gain).astype(bf16)
                for d in range(2):
                    grad = (scale[d] * g - pull[d] * y[d]).astype(bf16)
                    self.dy[s, d, t, lanes_of(h)] = grad
                    total = jnp.sum(grad.astype(f32) * (y[d] - direct), axis=1, keepdims=True)
                    given[d] = jnp.where(lane == h, total, given[d])
            for d in range(2):
                self.cols[d, s, t] = given[d]
        for h in range(heads):
            for d, grow in ((0, "grow_f"), (1, "grow_r")):
                left = (c_t * self.row(grow, s, h)).astype(bf16)
                self.put_rows(1, s, h, d, dot(left, self.dy[s, d, :, lanes_of(h)]))

    def local_grads(self, s):
        at, state = self.blocks(), self.state
        b_m, c_m = self.bc[s, 0, :, :state], self.bc[s, 1, :, :state]
        self.scores[...] = dot(b_m, c_m, NT)
        self.dscore[s] = jnp.zeros_like(self.scores)
        d_c = jnp.zeros((self.length, state), f32)
        above = iota2((LANES, LANES), 1) - iota2((LANES, LANES), 0)
        none = jnp.zeros((LANES, LANES), bf16)
        for h in range(self.heads):
            x_h = self.x[s, :, lanes_of(h)]
            d_f, d_r = self.dy[s, 0, :, lanes_of(h)], self.dy[s, 1, :, lanes_of(h)]
            p_f, p_r = dot(x_h, d_f, NT), dot(x_h, d_r, NT)
            f_rows, r_rows = [], []
            for i, t in enumerate(at):
                low, high = self.col("low", s, h, t), self.col("high", s, h, t)
                f_cols, r_cols = [], []
                for j in range(len(at)):
                    here = slice(i * LANES, (i + 1) * LANES), slice(j * LANES, (j + 1) * LANES)
                    to_f = lambda: self.row("cum", s, h)[:, here[1]] - low
                    to_r = lambda: high - self.row("exc", s, h)[:, here[1]]
                    power = to_f() if i < j else to_r() if i > j else jnp.minimum(to_f(), to_r())
                    decay = jnp.exp(power)
                    weight = decay * self.scores[here]
                    if i < j:
                        picked = p_f[here]
                        f_cols.append(weight.astype(bf16))
                        r_cols.append(none)
                    elif i > j:
                        picked = p_r[here]
                        f_cols.append(none)
                        r_cols.append(weight.astype(bf16))
                    else:
                        picked = jnp.where(above >= 0, p_f[here], 0.0) + jnp.where(above <= 0, p_r[here], 0.0)
                        f_cols.append(jnp.where(above >= 0, weight, 0.0).astype(bf16))
                        r_cols.append(jnp.where(above <= 0, weight, 0.0).astype(bf16))
                    self.dscore[s, t, here[1]] += decay * picked
                f_rows.append(jnp.concatenate(f_cols, axis=1))
                r_rows.append(jnp.concatenate(r_cols, axis=1))
            self.y[s, 0, :, lanes_of(h)] = dot(jnp.concatenate(f_rows, axis=0), d_f)
            self.y[s, 1, :, lanes_of(h)] = dot(jnp.concatenate(r_rows, axis=0), d_r)
            whole = pl.ds(0, self.length)
            d_c += dot(d_f, self.take_rows(self.fin, 0, s, h, 0), NT) * self.col("grow_f", s, h, whole)
            d_c += dot(d_r, self.take_rows(self.fin, 0, s, h, 1), NT) * self.col("grow_r", s, h, whole)
        self.carried[s, :, :state] = d_c

    def finish_grads(self, s):
        length, heads, state = self.length, self.heads, self.state
        at = self.blocks()
        b_m, c_m = self.bc[s, 0, :, :state], self.bc[s, 1, :, :state]
        lane = iota2((LANES, LANES), 1)
        lane_row = iota2((1, LANES), 1)
        zero = jnp.zeros((LANES, LANES), f32)
        into = [[zero for _ in at] for _ in range(2)]
        total = jnp.zeros((1, LANES), f32)
        d_b = jnp.zeros((length, state), f32)
        ends = jnp.exp(self.end_row[s])
        whole = pl.ds(0, length)
        for h in range(heads):
            x_h = self.x[s, :, lanes_of(h)]
            s_f, s_r = (self.take_rows(self.fin, 0, s, h, d).astype(f32) for d in range(2))
            in_f, in_r = (self.take_rows(self.fin, 1, s, h, d) for d in range(2))
            own, own_r = (self.take_rows(self.par, d, s, h, d).astype(f32) for d in range(2))
            tail_f, tail_r = self.col("tail_f", s, h, whole), self.col("tail_r", s, h, whole)
            u_f, u_r = dot(b_m, in_f), dot(b_m, in_r)
            d_b += dot(x_h, in_f, NT) * tail_f + dot(x_h, in_r, NT) * tail_r
            for i, t in enumerate(at):
                cut = slice(i * LANES, (i + 1) * LANES)
                x = self.x[s, t, lanes_of(h)].astype(f32)
                u = [
                    self.y[s, 0, t, lanes_of(h)] + tail_f[cut] * u_f[cut],
                    self.y[s, 1, t, lanes_of(h)] + tail_r[cut] * u_r[cut],
                ]
                skipped = self.dy[s, 0, t, lanes_of(h)].astype(f32) + self.dy[s, 1, t, lanes_of(h)].astype(f32)
                rows = pl.ds(s * length + i * LANES, LANES)
                self.dx[rows, lanes_of(h)] = (u[0] + u[1] + self.skip[:, h : h + 1] * skipped).astype(bf16)
                for d in range(2):
                    into[d][i] = jnp.where(lane == h, jnp.sum(x * u[d], axis=1, keepdims=True), into[d][i])
            decay = ends[:, h : h + 1]
            a_f, a_r = in_f.astype(f32), in_r.astype(f32)
            ending = a_f * (decay * s_f + own) + s_r * (decay * a_r + own_r)
            ended = jnp.sum(jnp.sum(ending, axis=0, keepdims=True), axis=1, keepdims=True)
            total = jnp.where(lane_row == h, ended, total)
        into_f, into_r = (jnp.concatenate(rows, axis=0) for rows in into)
        d_cum = self.cols[0, s] - into_f
        d_exc = into_r - self.cols[1, s]
        upper = (iota2((length, length), 0) <= iota2((length, length), 1)).astype(bf16)
        d_la = exact_dot(upper, d_cum + d_exc, heads) - d_exc + total
        d_raw = (into_f + into_r) * self.keep[1, s] - self.keep[0, s] * d_la
        d_raw = jnp.where(iota2((length, LANES), 1) < heads, d_raw, 0.0)
        scores = self.dscore[s].astype(bf16)
        d_b += dot(scores, c_m)
        d_c = self.carried[s, :, :state] + dot(scores, b_m, TN)
        tail = jnp.concatenate([d_raw[:, : LANES - 2 * state], d_b, d_c], axis=1)
        self.tail[pl.ds(s * length, length)] = tail.astype(bf16)

    def pair(self, which, k):
        length = self.length
        lower, upper = k * CHUNK, self.width - CHUNK - k * CHUNK
        first = jnp.where(self.mine == 0, lower, upper)
        other = lower + upper - first

        def product(start):
            at = chunk_at(start)
            if which == 0:
                return dot(self.z[...], self.wo[:, at])
            return dot(self.dx[...], self.wv[at, :], NT) + dot(self.tail[...], self.side[:, at])

        kept, away = product(first), product(other)
        turned = jnp.concatenate([kept[length:], away[length:]], axis=0).astype(bf16)
        turned = dot(turned, mirror_matrix())
        snd = self.out_snd if which == 0 else self.dh_snd
        snd[k] = (away[:length] + turned[:length]).astype(bf16)
        self.mp_copy(which, k).start()
        self.hold[which, k] = kept[:length] + turned[length:]

    def settle(self, which):
        rcv, out = (self.out_rcv, self.out) if which == 0 else (self.dh_rcv, self.dh)
        for k in range(self.chunks):
            self.mp_copy(which, k).wait()
            at = jnp.where(self.mine == 0, k, self.chunks - 1 - k)
            out[:, chunk_at(at * CHUNK)] = (self.hold[which, k] + rcv[k].astype(f32)).astype(bf16)


def layer_kernel(sizes, *refs):
    layer = Layer(sizes, refs + (pltpu.get_barrier_semaphore(),))
    length, inner = layer.length, layer.inner
    hidden_load, value_load, cot_load, out_load = layer.loads()
    for load in (hidden_load, value_load, cot_load, out_load):
        load.start()
    layer.greet()
    layer.side_weights()
    hidden_load.wait()
    layer.flip_into(layer.src)
    layer.prepare()
    for s in range(2):
        layer.end_row[s] = layer.cols[0, s, length - 1 : length]
    layer.meet()
    layer.start_decays()
    value_load.wait()

    def values(s):
        def one(k, none):
            at = chunk_at(k * CHUNK)
            layer.x[s, :, at] = dot(layer.src[pl.ds(s * length, length)], layer.wv[:, at]).astype(bf16)
            return none

        lax.fori_loop(0, inner // CHUNK, one, 0)

    def output_grads(k, none):
        at = chunk_at(k * CHUNK)
        both = dot(layer.grd[...], layer.wo[at, :], NT)
        layer.dz[0, :, at] = jnp.where(known, both[:length], 0.0).astype(bf16)
        layer.dz[1, :, at] = jnp.where(known, both[length:], 0.0).astype(bf16)
        return none

    for s in range(2):
        values(s)
        layer.ends(s)
        layer.begin(0, s)
    cot_load.wait()
    layer.flip_into(layer.grd)
    layer.finish_decays()
    layer.own_decays()
    layer.spread(0, 0)
    known = jnp.where(layer.ids[...] != 4, 1.0, 0.0)
    known = jnp.broadcast_to(known, (8, length)).T[:, :1] > 0.5
    out_load.wait()
    lax.fori_loop(0, inner // CHUNK, output_grads, 0)
    layer.spread(0, 1)
    layer.local_outputs(0)
    layer.send_home(0, 0)
    layer.local_outputs(1)
    layer.send_home(0, 1)
    layer.arrive(0, 0)
    layer.finish_outputs(0)
    layer.begin(1, 0)
    layer.arrive(0, 1)
    layer.finish_outputs(1)
    layer.begin(1, 1)
    layer.spread(1, 0)
    pairs = range(layer.chunks)
    half = layer.chunks // 2
    for k in pairs[:half]:
        layer.pair(0, k)
    layer.spread(1, 1)
    for k in pairs[half:]:
        layer.pair(0, k)
    layer.send_home(1, 0)
    layer.local_grads(0)
    layer.send_home(1, 1)
    layer.local_grads(1)
    layer.arrive(1, 0)
    layer.finish_grads(0)
    layer.arrive(1, 1)
    layer.finish_grads(1)
    for k in pairs:
        layer.pair(1, k)
    layer.settle(0)
    layer.settle(1)


def per_device(
    hidden, ids, w_value, w_bc, w_step, step_bias, decay_log, skip, norm_gain, w_out, cotangent
):
    length, width = hidden.shape
    heads, inner, state = w_step.shape[1], w_value.shape[1], w_bc.shape[2] // 2
    count, parts = lax.axis_size("seq"), lax.axis_size("mp")
    assert w_bc.shape[1] == 1 and inner == heads * LANES
    group = 1
    while 4 * group * group <= count:
        group *= 2
    assert count % group == 0 and heads % group == 0 and parts == 2
    planes, each = count // group, heads // group
    rows = each * state
    share = width // parts
    chunks = share // CHUNK
    vmem, anywhere = pl.BlockSpec(memory_space=pltpu.VMEM), pl.BlockSpec(memory_space=pl.ANY)
    parcel = (2, 2, group, 2, rows, LANES)
    travel = (chunks, length, CHUNK)
    sem = pltpu.SemaphoreType.DMA
    scratch = [
        pltpu.VMEM((2 * length, width), bf16),
        pltpu.VMEM((2 * length, width), bf16),
        pltpu.VMEM(w_value.shape, bf16),
        pltpu.VMEM(w_out.shape, bf16),
        pltpu.VMEM((LANES, width), bf16),
        pltpu.VMEM((2, length, inner), bf16),
        pltpu.VMEM((2, length, inner), bf16),
        pltpu.VMEM((2, 2, length, inner), f32),
        pltpu.VMEM((2 * length, inner), bf16),
        pltpu.VMEM((2, 2, length, inner), bf16),
        pltpu.VMEM((2 * length, inner), bf16),
        pltpu.VMEM((2 * length, LANES), bf16),
        pltpu.VMEM((2, length, LANES), f32),
        pltpu.VMEM((len(COLUMNS), 2, length, LANES), f32),
        pltpu.VMEM((len(COLUMNS), 2, heads, length), f32),
        pltpu.VMEM((2, 2, length, LANES), bf16),
        pltpu.VMEM((length, length), f32),
        pltpu.VMEM((2, length, length), f32),
        pltpu.VMEM((2, length, LANES), f32),
        pltpu.VMEM((2, 2 * state, length), f32),
        pltpu.VMEM((2, 2, length, LANES), f32),
        pltpu.VMEM((2, 1, LANES), f32),
        pltpu.VMEM((1, LANES), f32),
        pltpu.VMEM((count, 1, LANES), f32),
        pltpu.VMEM((2, each, count, LANES), f32),
        pltpu.VMEM((2, each, planes, LANES), f32),
        pltpu.VMEM(parcel, bf16),
        pltpu.VMEM(parcel, bf16),
        pltpu.VMEM((2, 2, 2, rows, LANES), bf16),
        pltpu.VMEM((2, 2, planes, rows, LANES), bf16),
        pltpu.VMEM(parcel, bf16),
        pltpu.VMEM(parcel, bf16),
        pltpu.VMEM(travel, bf16),
        pltpu.VMEM(travel, bf16),
        pltpu.VMEM(travel, bf16),
        pltpu.VMEM(travel, bf16),
        pltpu.VMEM((2,) + travel, f32),
        sem((4,)),
        sem((2, count)),
        sem((2, 4, group)),
        sem((2, 4, planes)),
        sem((2, 4, group)),
        sem((2, 2, chunks)),
    ]
    sizes = (length, width, inner, heads, state, count, group, parts)
    return pl.pallas_call(
        partial(layer_kernel, sizes),
        in_specs=[anywhere] * 4 + [vmem] * 7,
        out_specs=(vmem, vmem),
        out_shape=(jax.ShapeDtypeStruct((length, share), bf16),) * 2,
        scratch_shapes=scratch,
        compiler_params=pltpu.CompilerParams(
            collective_id=0, has_side_effects=True, vmem_limit_bytes=52 * 1024 * 1024
        ),
    )(
        hidden, cotangent, w_value, w_out, ids[None], w_step.T, w_bc.reshape(width, -1).T,
        step_bias[None], decay_log[None], skip[None], norm_gain[None],
    )


def solution(mesh):
    in_specs = (
        P("seq", None),
        P("seq"),
        P(None, "mp"),
        P(None, "mp", None),
        P(None, "mp"),
        P("mp"),
        P("mp"),
        P("mp"),
        P("mp"),
        P("mp", None),
        P("seq", None),
    )
    out_specs = (P("seq", "mp"), P("seq", "mp"))
    return jax.shard_map(
        per_device, mesh=mesh, in_specs=in_specs, out_specs=out_specs, check_vma=False
    )
```

time: 71.3 us -> 64 us (0.90)
  Pallas kernels: 66.7 us -> 56.4 us
  local copies, waits for them, and re-layouts: 3.74 us -> 6.62 us
    pallas_call x1, Pallas kernels: 66.7 us -> 56.4 us  [per_device(): pl.pallas_call(partial(layer_kernel, sizes), in_specs=[anywhere] * 4 + [v...]
    unnamed x2 -> x16, local copies, waits for them, and re-layouts: 3.74 us -> 6.62 us
where the time goes in v2:
time: 64 us; the launch traced here: 63.7 us
  Pallas kernels  56.4 us (88%)
  local copies, waits for them, and re-layouts  6.62 us (10%)
  between operations  0.66 us (1%)
    pallas_call x1, Pallas kernels, per_device(): pl.pallas_call(partial(layer_kernel, sizes), in_specs=[anywhere] * 4 + [v...  56.4 us
    unnamed x16, local copies, waits for them, and re-layouts  6.62 us

profile of v2, /device:TPU:0, one launch (start us, length us, event | category | flops | bytes accessed | tf_op | source)
XLA Modules:
  0.0 63.7 jit_solution(18002347343575641667)
XLA Ops:
  0.6 0.0 copy-start
  0.6 0.9 %copy-done = bf16[2048,1,64]{0,2,1:T(8,128)(2,1)S(1)} copy-done((bf16[2048,1,64]{0,2,1:T(8,128)(2,1)S(1)}, bf16[2048,1,64]{0,2,1:T(8,128)(2,1)}, u32[]{:S(2)}) %copy-start) | copy-done | bytes 262168
  1.6 0.0 copy-start.1
  1.6 0.8 %copy-done.1 = bf16[2048,8]{0,1:T(8,128)(2,1)S(1)} copy-done((bf16[2048,8]{0,1:T(8,128)(2,1)S(1)}, bf16[2048,8]{0,1:T(8,128)(2,1)}, u32[]{:S(2)}) %copy-start.1) | copy-done | bytes 32792
  2.3 0.0 copy-start.2
  2.3 0.7 %copy-done.2 = f32[1024]{0:T(1024)S(1)} copy-done((f32[1024]{0:T(1024)S(1)}, f32[1024]{0:T(1024)}, u32[]{:S(2)}) %copy-start.2) | copy-done | bytes 4120
  3.0 0.0 copy-start.3
  3.0 0.7 %copy-done.3 = s32[256]{0:T(256)S(1)} copy-done((s32[256]{0:T(256)S(1)}, s32[256]{0:T(256)}, u32[]{:S(2)}) %copy-start.3) | copy-done | bytes 1048
  3.7 0.0 copy-start.4
  3.7 0.7 %copy-done.4 = f32[8]{0:T(128)S(1)} copy-done((f32[8]{0:T(128)S(1)}, f32[8]{0:T(128)}, u32[]{:S(2)}) %copy-start.4) | copy-done | bytes 56
  4.4 0.0 copy-start.5
  4.4 0.7 %copy-done.5 = f32[8]{0:T(128)S(1)} copy-done((f32[8]{0:T(128)S(1)}, f32[8]{0:T(128)}, u32[]{:S(2)}) %copy-start.5) | copy-done | bytes 56
  5.0 0.0 copy-start.6
  5.0 0.7 %copy-done.6 = f32[8]{0:T(128)S(1)} copy-done((f32[8]{0:T(128)S(1)}, f32[8]{0:T(128)}, u32[]{:S(2)}) %copy-start.6) | copy-done | bytes 56
  5.7 56.4 %shard_map.122 = (bf16[256,1024]{1,0:T(8,128)(2,1)S(1)}, bf16[256,1024]{1,0:T(8,128)(2,1)S(1)}) custom-call(bf16[256,2048]{1,0:T(8,128)(2,1)} %refs_0_.1, bf16[256,2048]{1,0:T(8,128)(2,1)} %refs_1_.1, bf16[2048,1024]{1,0:T(8,128)(2,1)} %refs_2_.1, bf16[1024,2048]{1,0:T(8,128)(2,1)} %refs_3_.1, s32[1,256]{1,0:T(1,128)S(1)} %bitcast.12, ...), custom_call_target="tpu_custom_call" | custom-call | tf_op jit(solution)/shard_map/pallas_call | solution.py:623
  62.1 0.8 %copy.15 = bf16[256,1024]{1,0:T(8,128)(2,1)} copy(bf16[256,1024]{1,0:T(8,128)(2,1)S(1)} %get-tuple-element.4) | data formatting | bytes 1048576
  62.9 0.8 %copy.16 = bf16[256,1024]{1,0:T(8,128)(2,1)} copy(bf16[256,1024]{1,0:T(8,128)(2,1)S(1)} %get-tuple-element.5) | data formatting | bytes 1048576
Async XLA Ops:
  0.6 1.0 %copy-start = (bf16[2048,1,64]{0,2,1:T(8,128)(2,1)S(1)}, bf16[2048,1,64]{0,2,1:T(8,128)(2,1)}, u32[]{:S(2)}) copy-start(bf16[2048,1,64]{0,2,1:T(8,128)(2,1)} %param.14) | copy-start | bytes 786436
  1.6 0.8 %copy-start.1 = (bf16[2048,8]{0,1:T(8,128)(2,1)S(1)}, bf16[2048,8]{0,1:T(8,128)(2,1)}, u32[]{:S(2)}) copy-start(bf16[2048,8]{0,1:T(8,128)(2,1)} %param.15) | copy-start | bytes 98308
  2.3 0.7 %copy-start.2 = (f32[1024]{0:T(1024)S(1)}, f32[1024]{0:T(1024)}, u32[]{:S(2)}) copy-start(f32[1024]{0:T(1024)} %param.19) | copy-start | bytes 12292
  3.0 0.7 %copy-start.3 = (s32[256]{0:T(256)S(1)}, s32[256]{0:T(256)}, u32[]{:S(2)}) copy-start(s32[256]{0:T(256)} %param.12) | copy-start | bytes 3076
  3.7 0.7 %copy-start.4 = (f32[8]{0:T(128)S(1)}, f32[8]{0:T(128)}, u32[]{:S(2)}) copy-start(f32[8]{0:T(128)} %param.16) | copy-start | bytes 100
  4.4 0.7 %copy-start.5 = (f32[8]{0:T(128)S(1)}, f32[8]{0:T(128)}, u32[]{:S(2)}) copy-start(f32[8]{0:T(128)} %param.17) | copy-start | bytes 100
  5.0 0.7 %copy-start.6 = (f32[8]{0:T(128)S(1)}, f32[8]{0:T(128)}, u32[]{:S(2)}) copy-start(f32[8]{0:T(128)} %param.18) | copy-start | bytes 100

commit v3 on v2

--- a/solution.py
+++ b/solution.py
@@ -11,6 +11,7 @@
 epsilon = 1e-05
 LANES = 128
 CHUNK = 256
+STRIP = 32
 NN = (((1,), (0,)), ((), ()))
 NT = (((1,), (1,)), ((), ()))
 TN = (((0,), (0,)), ((), ()))
@@ -18,12 +19,13 @@
 COLUMNS = ("cum", "exc", "low", "high", "grow_f", "grow_r", "tail_f", "tail_r")
 
 NAMES = (
-    "hidden_hbm", "cot_hbm", "wv_hbm", "wo_hbm", "ids", "step_t", "bc_t", "bias", "decay", "skip",
-    "gain", "out", "dh", "src", "grd", "wv", "wo", "side", "x", "dz", "y", "z", "dy", "dx", "tail",
-    "aux", "cols", "rows", "bc", "scores", "dscore", "carried", "bct", "keep", "end_row", "dec_row",
-    "dec_got", "dec", "plane_dec", "par", "got", "agg", "far", "back", "fin", "out_snd", "out_rcv",
-    "dh_snd", "dh_rcv", "hold", "load_sem", "dec_sem", "go_sem", "far_sem", "home_sem", "mp_sem",
-    "barrier",
+    "hidden_hbm", "cot_hbm", "wv_hbm", "wo_hbm", "ids_hbm", "step_hbm", "bc_hbm", "bias_hbm",
+    "decay_hbm", "skip_hbm", "gain_hbm", "out", "dh", "src", "grd", "wv", "wo", "side", "x", "g", "direct", "wide", "grown",
+    "tailed", "prod", "pick", "gather", "y", "z", "dy", "dx", "tail", "aux", "cols", "rows", "bc",
+    "scores", "dscore", "carried", "bct", "keep", "end_row", "dec_row", "dec_got", "dec", "plane_dec",
+    "par", "got", "agg", "far", "back", "fin", "out_snd", "out_rcv", "dh_snd", "dh_rcv", "hold",
+    "load_sem", "dec_sem", "go_sem", "far_sem", "home_sem", "mp_sem", "small_sem", "ids", "step_t", "bc_t", "bias",
+    "decay", "skip", "gain", "barrier",
 )
 
 
@@ -47,13 +49,17 @@
     return pl.ds(h * LANES, LANES)
 
 
-def exact_dot(matrix, value, used):
+def thirds(value, used):
+    value = jnp.where(iota2(value.shape, 1) < used, value, 0.0)
     hi = value.astype(bf16).astype(f32)
     rest = value - hi
     mid = rest.astype(bf16).astype(f32)
     low = (rest - mid).astype(bf16).astype(f32)
-    packed = hi + pltpu.roll(mid, used, 1) + pltpu.roll(low, 2 * used, 1)
-    result = dot(matrix, packed.astype(bf16))
+    return (hi + pltpu.roll(mid, used, 1) + pltpu.roll(low, 2 * used, 1)).astype(bf16)
+
+
+def exact_dot(matrix, value, used):
+    result = dot(matrix, thirds(value, used))
     result += pltpu.roll(result, LANES - used, 1) + pltpu.roll(result, LANES - 2 * used, 1)
     return jnp.where(iota2(value.shape, 1) < used, result, 0.0)
 
@@ -76,6 +82,13 @@
         bottom = self.grd.at[pl.ds(0, self.length)]
         pairs = [(self.hidden_hbm, top), (self.wv_hbm, self.wv), (self.cot_hbm, bottom), (self.wo_hbm, self.wo)]
         return [pltpu.make_async_copy(a, b, self.load_sem.at[i]) for i, (a, b) in enumerate(pairs)]
+
+    def small_loads(self):
+        pairs = [
+            (self.step_hbm, self.step_t), (self.bc_hbm, self.bc_t), (self.bias_hbm, self.bias),
+            (self.decay_hbm, self.decay), (self.skip_hbm, self.skip), (self.gain_hbm, self.gain), (self.ids_hbm, self.ids),
+        ]
+        return [pltpu.make_async_copy(a, b, self.small_sem.at[i]) for i, (a, b) in enumerate(pairs)]
 
     def peer(self, hop):
         return lax.rem(self.me + hop, self.count)
@@ -221,6 +234,13 @@
             tile = ref[pl.ds(0, self.length), pl.ds(k * CHUNK, CHUNK)]
             there = pl.ds(self.width - CHUNK - k * CHUNK, CHUNK)
             ref[pl.ds(self.length, self.length), there] = dot(tile, mirror).astype(bf16)
+
+    def constants(self):
+        across = iota2((LANES, self.inner), 0), iota2((LANES, self.inner), 1) // LANES
+        match = lax.rem(across[0], self.heads) == across[1]
+        self.pick[...] = jnp.where(match & (across[0] < 3 * self.heads), 1.0, 0.0).astype(bf16)
+        down = iota2((self.inner, LANES), 0) // LANES, iota2((self.inner, LANES), 1)
+        self.gather[...] = (down[0] == down[1]).astype(bf16)
 
     def side_weights(self):
         gap = LANES - self.heads - 2 * self.state
@@ -306,60 +326,74 @@
                 low_rows.append(jnp.concatenate(low_cols, axis=1))
                 high_rows.append(jnp.concatenate(high_cols, axis=1))
             both = dot(jnp.concatenate(low_rows + high_rows, axis=0), self.x[s, :, lanes_of(h)])
-            self.y[s, 0, :, lanes_of(h)] = both[: self.length]
-            self.y[s, 1, :, lanes_of(h)] = both[self.length :]
+            direct = self.skip[:, h : h + 1] * self.x[s, :, lanes_of(h)].astype(f32)
+            self.direct[s, :, lanes_of(h)] = direct
+            self.y[s, 0, :, lanes_of(h)] = both[: self.length] + direct
+            self.y[s, 1, :, lanes_of(h)] = both[self.length :] + direct
+        for d, name in ((0, "grow_f"), (1, "grow_r")):
+            self.widen(name, s, d)
+
+    def widen(self, name, s, d):
+        self.wide[s, d] = dot(thirds(self.cols[COLUMNS.index(name), s], self.heads), self.pick[...])
+
+    def strips(self):
+        return [(r, pl.ds(r, STRIP)) for r in range(0, self.length, STRIP)]
+
+    def states(self, e, s, d):
+        return jnp.concatenate([self.take_rows(self.fin, e, s, h, d) for h in range(self.heads)], axis=1)
 
     def finish_outputs(self, s):
         length, heads, state = self.length, self.heads, self.state
-        at = self.blocks()
         c_m = self.bc[s, 1, :, :state]
-        c_t = self.bct[s, state:]
-        zero = jnp.zeros((LANES, LANES), f32)
-        squares = [[zero for _ in at] for _ in range(2)]
-        pulls = [[zero for _ in at] for _ in range(2)]
-        for h in range(heads):
-            carried = [dot(c_m, self.take_rows(self.fin, 0, s, h, d)) for d in range(2)]
-            for i, t in enumerate(at):
-                g = self.dz[s, t, lanes_of(h)].astype(f32) * self.gain[:, lanes_of(h)]
-                direct = self.skip[:, h : h + 1] * self.x[s, t, lanes_of(h)].astype(f32)
-                for d, grow in ((0, "grow_f"), (1, "grow_r")):
-                    y = self.y[s, d, t, lanes_of(h)] + self.col(grow, s, h, t) * carried[d][i * LANES : (i + 1) * LANES]
-                    y += direct
+        carried = [dot(c_m, self.states(0, s, d)) for d in range(2)]
+        zero = jnp.zeros((STRIP, LANES), f32)
+        share = 1.0 / (heads * LANES)
+        factors = []
+        for r, t in self.strips():
+            squares, pulls = [zero, zero], [zero, zero]
+            for h in range(heads):
+                g = self.g[s, t, lanes_of(h)]
+                for d in range(2):
+                    here = carried[d][r : r + STRIP, h * LANES : (h + 1) * LANES]
+                    y = self.y[s, d, t, lanes_of(h)] + self.wide[s, d, t, lanes_of(h)] * here
                     self.y[s, d, t, lanes_of(h)] = y
-                    squares[d][i] += y * y
-                    pulls[d][i] += g * y
-        share = 1.0 / (heads * LANES)
-        lane = iota2((LANES, LANES), 1)
-        for i, t in enumerate(at):
-            scale = [lax.rsqrt(jnp.sum(squares[d][i], axis=1, keepdims=True) * share + epsilon) for d in range(2)]
-            means = [scale[d] * jnp.sum(pulls[d][i], axis=1, keepdims=True) * share for d in range(2)]
-            pull = [scale[d] * scale[d] * means[d] for d in range(2)]
-            given = [zero, zero]
+                    squares[d] += y * y
+                    pulls[d] += g * y
+            scale = [lax.rsqrt(jnp.sum(q, axis=1, keepdims=True) * share + epsilon) for q in squares]
+            means = [scale[d] * jnp.sum(pulls[d], axis=1, keepdims=True) * share for d in range(2)]
+            factors.append((scale, [scale[d] * scale[d] * means[d] for d in range(2)]))
+        for (r, t), (scale, pull) in zip(self.strips(), factors):
             for h in range(heads):
-                gain = self.gain[:, lanes_of(h)]
-                g = self.dz[s, t, lanes_of(h)].astype(f32) * gain
-                direct = self.skip[:, h : h + 1] * self.x[s, t, lanes_of(h)].astype(f32)
+                g = self.g[s, t, lanes_of(h)]
+                direct = self.direct[s, t, lanes_of(h)]
                 y = [self.y[s, d, t, lanes_of(h)] for d in range(2)]
-                rows = pl.ds(s * length + i * LANES, LANES)
-                self.z[rows, lanes_of(h)] = ((y[0] * scale[0] + y[1] * scale[1]) * gain).astype(bf16)
+                z = (y[0] * scale[0] + y[1] * scale[1]) * self.gain[:, lanes_of(h)]
+                self.z[pl.ds(s * length + r, STRIP), lanes_of(h)] = z.astype(bf16)
                 for d in range(2):
                     grad = (scale[d] * g - pull[d] * y[d]).astype(bf16)
                     self.dy[s, d, t, lanes_of(h)] = grad
-                    total = jnp.sum(grad.astype(f32) * (y[d] - direct), axis=1, keepdims=True)
-                    given[d] = jnp.where(lane == h, total, given[d])
-            for d in range(2):
-                self.cols[d, s, t] = given[d]
-        for h in range(heads):
-            for d, grow in ((0, "grow_f"), (1, "grow_r")):
-                left = (c_t * self.row(grow, s, h)).astype(bf16)
-                self.put_rows(1, s, h, d, dot(left, self.dy[s, d, :, lanes_of(h)]))
+                    grad = grad.astype(f32)
+                    self.grown[s, d, t, lanes_of(h)] = (self.wide[s, d, t, lanes_of(h)] * grad).astype(bf16)
+                    self.prod[s, d, t, lanes_of(h)] = (grad * (y[d] - direct)).astype(bf16)
+        c_t = self.bct[s, state:].astype(bf16)
+        for d in range(2):
+            own = dot(c_t, self.grown[s, d])
+            for h in range(heads):
+                self.put_rows(1, s, h, d, own[:, h * LANES : (h + 1) * LANES])
+
+    def between(self, s):
+        for d, name in ((0, "tail_f"), (1, "tail_r")):
+            self.cols[d, s] = dot(self.prod[s, d], self.gather[...])
+            self.widen(name, s, d)
+            self.tailed[s, d] = (self.wide[s, d] * self.x[s].astype(f32)).astype(bf16)
+        carried = [dot(self.grown[s, d], self.states(0, s, d), NT) for d in range(2)]
+        self.carried[s, :, : self.state] = carried[0] + carried[1]
 
     def local_grads(self, s):
         at, state = self.blocks(), self.state
         b_m, c_m = self.bc[s, 0, :, :state], self.bc[s, 1, :, :state]
         self.scores[...] = dot(b_m, c_m, NT)
         self.dscore[s] = jnp.zeros_like(self.scores)
-        d_c = jnp.zeros((self.length, state), f32)
         above = iota2((LANES, LANES), 1) - iota2((LANES, LANES), 0)
         none = jnp.zeros((LANES, LANES), bf16)
         for h in range(self.heads):
@@ -394,49 +428,36 @@
                 r_rows.append(jnp.concatenate(r_cols, axis=1))
             self.y[s, 0, :, lanes_of(h)] = dot(jnp.concatenate(f_rows, axis=0), d_f)
             self.y[s, 1, :, lanes_of(h)] = dot(jnp.concatenate(r_rows, axis=0), d_r)
-            whole = pl.ds(0, self.length)
-            d_c += dot(d_f, self.take_rows(self.fin, 0, s, h, 0), NT) * self.col("grow_f", s, h, whole)
-            d_c += dot(d_r, self.take_rows(self.fin, 0, s, h, 1), NT) * self.col("grow_r", s, h, whole)
-        self.carried[s, :, :state] = d_c
 
     def finish_grads(self, s):
         length, heads, state = self.length, self.heads, self.state
-        at = self.blocks()
         b_m, c_m = self.bc[s, 0, :, :state], self.bc[s, 1, :, :state]
-        lane = iota2((LANES, LANES), 1)
         lane_row = iota2((1, LANES), 1)
-        zero = jnp.zeros((LANES, LANES), f32)
-        into = [[zero for _ in at] for _ in range(2)]
         total = jnp.zeros((1, LANES), f32)
-        d_b = jnp.zeros((length, state), f32)
         ends = jnp.exp(self.end_row[s])
-        whole = pl.ds(0, length)
+        inward = [self.states(1, s, d) for d in range(2)]
+        carried = [dot(b_m, inward[d]) for d in range(2)]
+        for r, t in self.strips():
+            for h in range(heads):
+                x = self.x[s, t, lanes_of(h)].astype(f32)
+                skipped = self.dy[s, 0, t, lanes_of(h)].astype(f32) + self.dy[s, 1, t, lanes_of(h)].astype(f32)
+                dx = self.skip[:, h : h + 1] * skipped
+                for d in range(2):
+                    here = carried[d][r : r + STRIP, h * LANES : (h + 1) * LANES]
+                    u = self.y[s, d, t, lanes_of(h)] + self.wide[s, d, t, lanes_of(h)] * here
+                    dx += u
+                    self.prod[s, d, t, lanes_of(h)] = (x * u).astype(bf16)
+                self.dx[pl.ds(s * length + r, STRIP), lanes_of(h)] = dx.astype(bf16)
+        d_b = dot(self.tailed[s, 0], inward[0], NT) + dot(self.tailed[s, 1], inward[1], NT)
         for h in range(heads):
-            x_h = self.x[s, :, lanes_of(h)]
             s_f, s_r = (self.take_rows(self.fin, 0, s, h, d).astype(f32) for d in range(2))
-            in_f, in_r = (self.take_rows(self.fin, 1, s, h, d) for d in range(2))
+            a_f, a_r = (self.take_rows(self.fin, 1, s, h, d).astype(f32) for d in range(2))
             own, own_r = (self.take_rows(self.par, d, s, h, d).astype(f32) for d in range(2))
-            tail_f, tail_r = self.col("tail_f", s, h, whole), self.col("tail_r", s, h, whole)
-            u_f, u_r = dot(b_m, in_f), dot(b_m, in_r)
-            d_b += dot(x_h, in_f, NT) * tail_f + dot(x_h, in_r, NT) * tail_r
-            for i, t in enumerate(at):
-                cut = slice(i * LANES, (i + 1) * LANES)
-                x = self.x[s, t, lanes_of(h)].astype(f32)
-                u = [
-                    self.y[s, 0, t, lanes_of(h)] + tail_f[cut] * u_f[cut],
-                    self.y[s, 1, t, lanes_of(h)] + tail_r[cut] * u_r[cut],
-                ]
-                skipped = self.dy[s, 0, t, lanes_of(h)].astype(f32) + self.dy[s, 1, t, lanes_of(h)].astype(f32)
-                rows = pl.ds(s * length + i * LANES, LANES)
-                self.dx[rows, lanes_of(h)] = (u[0] + u[1] + self.skip[:, h : h + 1] * skipped).astype(bf16)
-                for d in range(2):
-                    into[d][i] = jnp.where(lane == h, jnp.sum(x * u[d], axis=1, keepdims=True), into[d][i])
             decay = ends[:, h : h + 1]
-            a_f, a_r = in_f.astype(f32), in_r.astype(f32)
             ending = a_f * (decay * s_f + own) + s_r * (decay * a_r + own_r)
             ended = jnp.sum(jnp.sum(ending, axis=0, keepdims=True), axis=1, keepdims=True)
             total = jnp.where(lane_row == h, ended, total)
-        into_f, into_r = (jnp.concatenate(rows, axis=0) for rows in into)
+        into_f, into_r = (dot(self.prod[s, d], self.gather[...]) for d in range(2))
         d_cum = self.cols[0, s] - into_f
         d_exc = into_r - self.cols[1, s]
         upper = (iota2((length, length), 0) <= iota2((length, length), 1)).astype(bf16)
@@ -481,9 +502,13 @@
     layer = Layer(sizes, refs + (pltpu.get_barrier_semaphore(),))
     length, inner = layer.length, layer.inner
     hidden_load, value_load, cot_load, out_load = layer.loads()
-    for load in (hidden_load, value_load, cot_load, out_load):
+    small_loads = layer.small_loads()
+    for load in [hidden_load] + small_loads + [value_load, cot_load, out_load]:
         load.start()
     layer.greet()
+    layer.constants()
+    for load in small_loads:
+        load.wait()
     layer.side_weights()
     hidden_load.wait()
     layer.flip_into(layer.src)
@@ -505,8 +530,9 @@
     def output_grads(k, none):
         at = chunk_at(k * CHUNK)
         both = dot(layer.grd[...], layer.wo[at, :], NT)
-        layer.dz[0, :, at] = jnp.where(known, both[:length], 0.0).astype(bf16)
-        layer.dz[1, :, at] = jnp.where(known, both[length:], 0.0).astype(bf16)
+        for s in range(2):
+            dz = jnp.where(known, both[s * length : (s + 1) * length], 0.0).astype(bf16)
+            layer.g[s, :, at] = dz.astype(f32) * layer.gain[:, at]
         return none
 
     for s in range(2):
@@ -533,6 +559,7 @@
     layer.arrive(0, 1)
     layer.finish_outputs(1)
     layer.begin(1, 1)
+    layer.between(0)
     layer.spread(1, 0)
     pairs = range(layer.chunks)
     half = layer.chunks // 2
@@ -543,6 +570,7 @@
         layer.pair(0, k)
     layer.send_home(1, 0)
     layer.local_grads(0)
+    layer.between(1)
     layer.send_home(1, 1)
     layer.local_grads(1)
     layer.arrive(1, 0)
@@ -570,7 +598,7 @@
     rows = each * state
     share = width // parts
     chunks = share // CHUNK
-    vmem, anywhere = pl.BlockSpec(memory_space=pltpu.VMEM), pl.BlockSpec(memory_space=pl.ANY)
+    vmem, hbm = pl.BlockSpec(memory_space=pltpu.VMEM), pl.BlockSpec(memory_space=pltpu.HBM)
     parcel = (2, 2, group, 2, rows, LANES)
     travel = (chunks, length, CHUNK)
     sem = pltpu.SemaphoreType.DMA
@@ -581,7 +609,14 @@
         pltpu.VMEM(w_out.shape, bf16),
         pltpu.VMEM((LANES, width), bf16),
         pltpu.VMEM((2, length, inner), bf16),
-        pltpu.VMEM((2, length, inner), bf16),
+        pltpu.VMEM((2, length, inner), f32),
+        pltpu.VMEM((2, length, inner), f32),
+        pltpu.VMEM((2, 2, length, inner), f32),
+        pltpu.VMEM((2, 2, length, inner), bf16),
+        pltpu.VMEM((2, 2, length, inner), bf16),
+        pltpu.VMEM((2, 2, length, inner), bf16),
+        pltpu.VMEM((LANES, inner), bf16),
+        pltpu.VMEM((inner, LANES), bf16),
         pltpu.VMEM((2, 2, length, inner), f32),
         pltpu.VMEM((2 * length, inner), bf16),
         pltpu.VMEM((2, 2, length, inner), bf16),
@@ -618,11 +653,19 @@
         sem((2, 4, planes)),
         sem((2, 4, group)),
         sem((2, 2, chunks)),
+        sem((7,)),
+        pltpu.VMEM((1, length), jnp.int32),
+        pltpu.VMEM((heads, width), bf16),
+        pltpu.VMEM((2 * state, width), bf16),
+        pltpu.VMEM((1, heads), f32),
+        pltpu.VMEM((1, heads), f32),
+        pltpu.VMEM((1, heads), f32),
+        pltpu.VMEM((1, inner), f32),
     ]
     sizes = (length, width, inner, heads, state, count, group, parts)
     return pl.pallas_call(
         partial(layer_kernel, sizes),
-        in_specs=[anywhere] * 4 + [vmem] * 7,
+        in_specs=[hbm] * 11,
         out_specs=(vmem, vmem),
         out_shape=(jax.ShapeDtypeStruct((length, share), bf16),) * 2,
         scratch_shapes=scratch,
@@ -630,8 +673,13 @@
             collective_id=0, has_side_effects=True, vmem_limit_bytes=52 * 1024 * 1024
         ),
     )(
-        hidden, cotangent, w_value, w_out, ids[None], w_step.T, w_bc.reshape(width, -1).T,
-        step_bias[None], decay_log[None], skip[None], norm_gain[None],
+        *(
+            pltpu.with_memory_space_constraint(value, pltpu.HBM)
+            for value in (
+                hidden, cotangent, w_value, w_out, ids[None], w_step.T, w_bc.reshape(width, -1).T,
+                step_bias[None], decay_log[None], skip[None], norm_gain[None],
+            )
+        )
     )
 
 

time: 64 us -> 57.6 us (0.900)
  local copies, waits for them, and re-layouts: 6.62 us -> 1.59 us
  Pallas kernels: 56.4 us -> 55.3 us
    unnamed x16 -> x2, local copies, waits for them, and re-layouts: 6.62 us -> 1.59 us
    pallas_call x1, Pallas kernels: 56.4 us -> 55.3 us  [per_device(): pl.pallas_call(partial(layer_kernel, sizes), in_specs=[hbm] * 11, out_spe...]
where the time goes in v3:
time: 57.6 us; the launch traced here: 57.5 us
  Pallas kernels  55.3 us (96%)
  local copies, waits for them, and re-layouts  1.59 us (3%)
  between operations  0.64 us (1%)
    pallas_call x1, Pallas kernels, per_device(): pl.pallas_call(partial(layer_kernel, sizes), in_specs=[hbm] * 11, out_spe...  55.3 us
    unnamed x2, local copies, waits for them, and re-layouts  1.59 us

profile of v3, /device:TPU:0, one launch (start us, length us, event | category | flops | bytes accessed | tf_op | source)
XLA Modules:
  0.0 57.5 jit_solution(9661588909892683586)
XLA Ops:
  0.6 55.3 %shard_map.122 = (bf16[256,1024]{1,0:T(8,128)(2,1)S(1)}, bf16[256,1024]{1,0:T(8,128)(2,1)S(1)}) custom-call(bf16[256,2048]{1,0:T(8,128)(2,1)} %refs_0_.1, bf16[256,2048]{1,0:T(8,128)(2,1)} %refs_1_.1, bf16[2048,1024]{1,0:T(8,128)(2,1)} %refs_2_.1, bf16[1024,2048]{1,0:T(8,128)(2,1)} %refs_3_.1, s32[1,256]{1,0:T(1,128)} %bitcast.12, bf16[8,2048]{1,0:T(8,128)(2,1)} %bitcast.10, ...), custom_call_target="tpu_custom_call" | custom-call | tf_op jit(solution)/shard_map/pallas_call | solution.py:666
  55.9 0.8 %copy.15 = bf16[256,1024]{1,0:T(8,128)(2,1)} copy(bf16[256,1024]{1,0:T(8,128)(2,1)S(1)} %get-tuple-element.4) | data formatting | bytes 1048576
  56.7 0.8 %copy.16 = bf16[256,1024]{1,0:T(8,128)(2,1)} copy(bf16[256,1024]{1,0:T(8,128)(2,1)S(1)} %get-tuple-element.5) | data formatting | bytes 1048576

commit v4 on v3

--- a/solution.py
+++ b/solution.py
@@ -110,22 +110,16 @@
             device_id=device, device_id_type=MESH_ID,
         )
 
-    def decay_copy(self, hop):
-        return self.remote(self.dec_row, self.dec_got.at[self.me], self.dec_sem, (hop,), {"seq": self.peer(hop)})
-
-    def start_decays(self):
-        def one(hop, none):
-            self.decay_copy(hop).start()
-            return none
-
-        lax.fori_loop(1, self.count, one, 0)
-
-    def finish_decays(self):
-        def one(hop, none):
-            self.decay_copy(hop).wait()
-            return none
-
-        lax.fori_loop(1, self.count, one, 0)
+    def decay_copy(self, plane_hop, member_hop):
+        plane = lax.rem(self.plane + plane_hop, self.planes)
+        to = plane * self.group + lax.rem(self.member + member_hop, self.group)
+        return self.remote(self.dec_row, self.dec_got.at[self.me], self.dec_sem, (plane_hop, member_hop), {"seq": to})
+
+    def near_decays(self):
+        return [self.decay_copy(0, m) for m in range(1, self.group)]
+
+    def far_decays(self):
+        return [self.decay_copy(p, m) for p in range(1, self.planes) for m in range(self.group)]
 
     def gather_copies(self, e, s):
         for hop in range(1, self.group):
@@ -163,16 +157,28 @@
     def take_rows(self, ref, e, s, h, which):
         return ref[e, s, h // self.each, which, pl.ds(h % self.each * self.state, self.state)]
 
-    def own_decays(self):
+    def decays_of(self, rows, s, q):
+        table = jnp.concatenate(rows, axis=0)
+        head = s * self.heads + self.member * self.each + q
+        picked = jnp.sum(jnp.where(iota2(table.shape, 1) == head, table, 0.0), axis=1, keepdims=True)
+        return jnp.broadcast_to(picked, table.shape)
+
+    def take_near(self):
+        for copy in self.near_decays():
+            copy.wait()
         self.dec_got[self.me] = self.dec_row[...]
-        table = jnp.concatenate([self.dec_got[j] for j in range(self.count)], axis=0)
-        lane = iota2((self.count, LANES), 1)
+        rows = [self.dec_got[self.plane * self.group + m] for m in range(self.group)]
         for s in range(2):
             for q in range(self.each):
-                head = s * self.heads + self.member * self.each + q
-                picked = jnp.sum(jnp.where(lane == head, table, 0.0), axis=1, keepdims=True)
-                wide = jnp.broadcast_to(picked, (self.count, LANES))
-                self.dec[s, q] = wide
+                self.dec[s, q] = self.decays_of(rows, s, q)
+
+    def take_far(self):
+        for copy in self.far_decays():
+            copy.wait()
+        rows = [self.dec_got[j] for j in range(self.count)]
+        for s in range(2):
+            for q in range(self.each):
+                wide = self.decays_of(rows, s, q)
                 for p in range(self.planes):
                     product = wide[p * self.group : p * self.group + 1]
                     for m in range(1, self.group):
@@ -184,8 +190,7 @@
         at = pl.ds(q * self.state, self.state)
         for m in order:
             visit(m, at, total)
-            decay = self.dec[s, q, pl.ds(self.plane * self.group + m, 1)]
-            total = decay * total + self.got[e, s, m, which, at].astype(f32)
+            total = self.dec[s, q, m : m + 1] * total + self.got[e, s, m, which, at].astype(f32)
         return total
 
     def begin(self, e, s):
@@ -470,32 +475,30 @@
         tail = jnp.concatenate([d_raw[:, : LANES - 2 * state], d_b, d_c], axis=1)
         self.tail[pl.ds(s * length, length)] = tail.astype(bf16)
 
-    def pair(self, which, k):
+    def half(self, which, k, away):
         length = self.length
         lower, upper = k * CHUNK, self.width - CHUNK - k * CHUNK
-        first = jnp.where(self.mine == 0, lower, upper)
-        other = lower + upper - first
-
-        def product(start):
-            at = chunk_at(start)
+        here = jnp.where(self.mine == (1 if away else 0), lower, upper)
+        there = lower + upper - here
+
+        def product(s, start):
+            at, rows = chunk_at(start), pl.ds(s * length, length)
             if which == 0:
-                return dot(self.z[...], self.wo[:, at])
-            return dot(self.dx[...], self.wv[at, :], NT) + dot(self.tail[...], self.side[:, at])
-
-        kept, away = product(first), product(other)
-        turned = jnp.concatenate([kept[length:], away[length:]], axis=0).astype(bf16)
-        turned = dot(turned, mirror_matrix())
+                return dot(self.z[rows], self.wo[:, at])
+            return dot(self.dx[rows], self.wv[at, :], NT) + dot(self.tail[rows], self.side[:, at])
+
+        return product(0, here) + dot(product(1, there).astype(bf16), mirror_matrix())
+
+    def send(self, which, k):
         snd = self.out_snd if which == 0 else self.dh_snd
-        snd[k] = (away[:length] + turned[:length]).astype(bf16)
+        snd[k] = self.half(which, k, True).astype(bf16)
         self.mp_copy(which, k).start()
-        self.hold[which, k] = kept[:length] + turned[length:]
-
-    def settle(self, which):
+
+    def settle(self, which, k, kept):
         rcv, out = (self.out_rcv, self.out) if which == 0 else (self.dh_rcv, self.dh)
-        for k in range(self.chunks):
-            self.mp_copy(which, k).wait()
-            at = jnp.where(self.mine == 0, k, self.chunks - 1 - k)
-            out[:, chunk_at(at * CHUNK)] = (self.hold[which, k] + rcv[k].astype(f32)).astype(bf16)
+        self.mp_copy(which, k).wait()
+        at = jnp.where(self.mine == 0, k, self.chunks - 1 - k)
+        out[:, chunk_at(at * CHUNK)] = (kept + rcv[k].astype(f32)).astype(bf16)
 
 
 def layer_kernel(sizes, *refs):
@@ -516,7 +519,8 @@
     for s in range(2):
         layer.end_row[s] = layer.cols[0, s, length - 1 : length]
     layer.meet()
-    layer.start_decays()
+    for copy in layer.near_decays() + layer.far_decays():
+        copy.start()
     value_load.wait()
 
     def values(s):
@@ -539,35 +543,36 @@
         values(s)
         layer.ends(s)
         layer.begin(0, s)
+    layer.take_near()
+    layer.spread(0, 0)
     cot_load.wait()
     layer.flip_into(layer.grd)
-    layer.finish_decays()
-    layer.own_decays()
-    layer.spread(0, 0)
     known = jnp.where(layer.ids[...] != 4, 1.0, 0.0)
     known = jnp.broadcast_to(known, (8, length)).T[:, :1] > 0.5
     out_load.wait()
-    lax.fori_loop(0, inner // CHUNK, output_grads, 0)
+    middle = inner // CHUNK // 2
+    lax.fori_loop(0, middle, output_grads, 0)
     layer.spread(0, 1)
+    lax.fori_loop(middle, inner // CHUNK, output_grads, 0)
+    layer.take_far()
+    layer.send_home(0, 0)
     layer.local_outputs(0)
-    layer.send_home(0, 0)
+    layer.send_home(0, 1)
     layer.local_outputs(1)
-    layer.send_home(0, 1)
     layer.arrive(0, 0)
     layer.finish_outputs(0)
     layer.begin(1, 0)
     layer.arrive(0, 1)
     layer.finish_outputs(1)
     layer.begin(1, 1)
+    chunks = range(layer.chunks)
     layer.between(0)
     layer.spread(1, 0)
-    pairs = range(layer.chunks)
-    half = layer.chunks // 2
-    for k in pairs[:half]:
-        layer.pair(0, k)
+    layer.send(0, 0)
+    layer.send(0, 1)
     layer.spread(1, 1)
-    for k in pairs[half:]:
-        layer.pair(0, k)
+    layer.send(0, 2)
+    layer.send(0, 3)
     layer.send_home(1, 0)
     layer.local_grads(0)
     layer.between(1)
@@ -577,10 +582,14 @@
     layer.finish_grads(0)
     layer.arrive(1, 1)
     layer.finish_grads(1)
-    for k in pairs:
-        layer.pair(1, k)
-    layer.settle(0)
-    layer.settle(1)
+    for k in chunks:
+        layer.send(1, k)
+    for k in chunks:
+        layer.settle(0, k, layer.half(0, k, False))
+    for k in chunks:
+        layer.hold[k] = layer.half(1, k, False)
+    for k in chunks:
+        layer.settle(1, k, layer.hold[k])
 
 
 def per_device(
@@ -634,7 +643,7 @@
         pltpu.VMEM((2, 1, LANES), f32),
         pltpu.VMEM((1, LANES), f32),
         pltpu.VMEM((count, 1, LANES), f32),
-        pltpu.VMEM((2, each, count, LANES), f32),
+        pltpu.VMEM((2, each, group, LANES), f32),
         pltpu.VMEM((2, each, planes, LANES), f32),
         pltpu.VMEM(parcel, bf16),
         pltpu.VMEM(parcel, bf16),
@@ -646,9 +655,9 @@
         pltpu.VMEM(travel, bf16),
         pltpu.VMEM(travel, bf16),
         pltpu.VMEM(travel, bf16),
-        pltpu.VMEM((2,) + travel, f32),
+        pltpu.VMEM(travel, f32),
         sem((4,)),
-        sem((2, count)),
+        sem((2, planes, group)),
         sem((2, 4, group)),
         sem((2, 4, planes)),
         sem((2, 4, group)),

time: 57.6 us -> 55.7 us (0.967)
  Pallas kernels: 55.3 us -> 53.3 us
    pallas_call x1, Pallas kernels: 55.3 us -> 53.3 us  [per_device(): pl.pallas_call(partial(layer_kernel, sizes), in_specs=[hbm] * 11, out_spe...]
where the time goes in v4:
time: 55.7 us; the launch traced here: 55.6 us
  Pallas kernels  53.3 us (96%)
  local copies, waits for them, and re-layouts  1.59 us (3%)
  between operations  0.64 us (1%)
    pallas_call x1, Pallas kernels, per_device(): pl.pallas_call(partial(layer_kernel, sizes), in_specs=[hbm] * 11, out_spe...  53.3 us
    unnamed x2, local copies, waits for them, and re-layouts  1.59 us

profile of v4, /device:TPU:0, one launch (start us, length us, event | category | flops | bytes accessed | tf_op | source)
XLA Modules:
  0.0 55.6 jit_solution(12402757397319042651)
XLA Ops:
  0.6 53.3 %shard_map.122 = (bf16[256,1024]{1,0:T(8,128)(2,1)S(1)}, bf16[256,1024]{1,0:T(8,128)(2,1)S(1)}) custom-call(bf16[256,2048]{1,0:T(8,128)(2,1)} %refs_0_.1, bf16[256,2048]{1,0:T(8,128)(2,1)} %refs_1_.1, bf16[2048,1024]{1,0:T(8,128)(2,1)} %refs_2_.1, bf16[1024,2048]{1,0:T(8,128)(2,1)} %refs_3_.1, s32[1,256]{1,0:T(1,128)} %bitcast.12, bf16[8,2048]{1,0:T(8,128)(2,1)} %bitcast.10, ...), custom_call_target="tpu_custom_call" | custom-call | tf_op jit(solution)/shard_map/pallas_call | solution.py:675
  54.0 0.8 %copy.15 = bf16[256,1024]{1,0:T(8,128)(2,1)} copy(bf16[256,1024]{1,0:T(8,128)(2,1)S(1)} %get-tuple-element.4) | data formatting | bytes 1048576
  54.8 0.8 %copy.16 = bf16[256,1024]{1,0:T(8,128)(2,1)} copy(bf16[256,1024]{1,0:T(8,128)(2,1)S(1)} %get-tuple-element.5) | data formatting | bytes 1048576

commit v5 on v4

--- a/solution.py
+++ b/solution.py
@@ -568,11 +568,11 @@
     chunks = range(layer.chunks)
     layer.between(0)
     layer.spread(1, 0)
-    layer.send(0, 0)
-    layer.send(0, 1)
+    for k in chunks[: layer.chunks // 2]:
+        layer.send(0, k)
     layer.spread(1, 1)
-    layer.send(0, 2)
-    layer.send(0, 3)
+    for k in chunks[layer.chunks // 2 :]:
+        layer.send(0, k)
     layer.send_home(1, 0)
     layer.local_grads(0)
     layer.between(1)

time: 55.7 us -> 55.7 us (level)
  no operation moved by 1% of the time
where the time goes in v5:
time: 55.7 us; the launch traced here: 55.6 us
  Pallas kernels  53.3 us (96%)
  local copies, waits for them, and re-layouts  1.59 us (3%)
  between operations  0.64 us (1%)
    pallas_call x1, Pallas kernels, per_device(): pl.pallas_call(partial(layer_kernel, sizes), in_specs=[hbm] * 11, out_spe...  53.3 us
    unnamed x2, local copies, waits for them, and re-layouts  1.59 us

profile of v5, /device:TPU:0, one launch (start us, length us, event | category | flops | bytes accessed | tf_op | source)
XLA Modules:
  0.0 55.6 jit_solution(12402757397319042651)
XLA Ops:
  0.6 53.3 %shard_map.122 = (bf16[256,1024]{1,0:T(8,128)(2,1)S(1)}, bf16[256,1024]{1,0:T(8,128)(2,1)S(1)}) custom-call(bf16[256,2048]{1,0:T(8,128)(2,1)} %refs_0_.1, bf16[256,2048]{1,0:T(8,128)(2,1)} %refs_1_.1, bf16[2048,1024]{1,0:T(8,128)(2,1)} %refs_2_.1, bf16[1024,2048]{1,0:T(8,128)(2,1)} %refs_3_.1, s32[1,256]{1,0:T(1,128)} %bitcast.12, bf16[8,2048]{1,0:T(8,128)(2,1)} %bitcast.10, ...), custom_call_target="tpu_custom_call" | custom-call | tf_op jit(solution)/shard_map/pallas_call | solution.py:675
  54.0 0.8 %copy.15 = bf16[256,1024]{1,0:T(8,128)(2,1)} copy(bf16[256,1024]{1,0:T(8,128)(2,1)S(1)} %get-tuple-element.4) | data formatting | bytes 1048576
  54.8 0.8 %copy.16 = bf16[256,1024]{1,0:T(8,128)(2,1)} copy(bf16[256,1024]{1,0:T(8,128)(2,1)S(1)} %get-tuple-element.5) | data formatting | bytes 1048576
